TPU v7x, 256 devices: a whole 4x4x8 slice. The times are simulated.
256 devices in a mesh: sub: 32 (over y, z_lo, x), alt: 8 (over z_hi, core).
Axes of the slice: x: 4, y: 4, z: 8 (z_hi: 4, z_lo: 2; z = z_hi * 2 + z_lo), core: 2. Of those that a mesh axis runs over, the one named last changes fastest.
Arguments:
- cotangent: bfloat16 [4096, 4096], P('alt', 'sub'), may hold values from -180 to 180, as said below
- amplitude: bfloat16 [1024, 4096], P('alt', 'sub'), may hold values from 0.19921875 to 1
- phase: float32 [1024, 4096], P('alt', 'sub'), may hold values from -6 to 6
- position: float32 [2, 4096], P(None, 'sub'), may hold values from -1 to 1
- profile: float32 [16], P('alt'), may hold values from 0.35 to 15, as said below
- alt_weight: float32 [16], P('alt'), may hold values from 0.3 to 3
Outputs:
- phase_grad: float32 [1024, 4096], P('alt', 'sub')
- profile_grad: float32 [16], P('alt')
Inputs may be any that keep to these rules, and one draw needn't show every extreme that they name: `cotangent`: cotangent values of varying scale per subaperture. `profile`: positive sodium densities.
All inputs are finite; a program needn't handle non-finite values.
Results may differ from a plain program's by a relative error of at most 0.0003.
Values may be sent and summed in bfloat16 or wider, within the bound.
A program may use at most 64 MiB of HBM per device.

v0:
```python
import jax
import jax.numpy as jnp
from jax import lax
from jax.sharding import PartitionSpec as P

P_SIZE = 32
FIELD = 64


ELONG = 0.75


def dft_tables(size_pupil, size_field):
    rows = jnp.arange(size_field, dtype=jnp.int32)[:, None]
    cols = jnp.arange(size_pupil, dtype=jnp.int32)[None, :]
    angle = 2.0 * jnp.pi / size_field * (rows * cols % size_field).astype(jnp.float32)
    return (jnp.cos(angle), -jnp.sin(angle))


def spot_image(psi, ampl, table_re, table_im, size_pupil):
    high = lax.Precision.HIGHEST
    field_re = ampl * jnp.cos(psi)
    field_im = ampl * jnp.sin(psi)
    first_re = jnp.einsum("kj,ajs->aks", table_re, field_re, precision=high) - jnp.einsum(
        "kj,ajs->aks", table_im, field_im, precision=high
    )
    first_im = jnp.einsum("kj,ajs->aks", table_re, field_im, precision=high) + jnp.einsum(
        "kj,ajs->aks", table_im, field_re, precision=high
    )
    final_re = jnp.einsum("ka,ams->kms", table_re, first_re, precision=high) - jnp.einsum(
        "ka,ams->kms", table_im, first_im, precision=high
    )
    final_im = jnp.einsum("ka,ams->kms", table_re, first_im, precision=high) + jnp.einsum(
        "ka,ams->kms", table_im, first_re, precision=high
    )
    return (final_re * final_re + final_im * final_im) / (size_pupil * size_pupil)


def run_bins(
    grad_rows, ampl_rows, phase_rows, coords_xy, densities, weights, first_bin, nbins_all, group
):
    count = phase_rows.shape[1]
    total_bins = densities.shape[0]
    blocks = total_bins // group
    grad_img = grad_rows.astype(jnp.float32).reshape(FIELD, FIELD, count)
    ampl = ampl_rows.astype(jnp.float32).reshape(P_SIZE, P_SIZE, count)
    phases = phase_rows.reshape(P_SIZE, P_SIZE, count)
    table_re, table_im = dft_tables(P_SIZE, FIELD)
    coord = jnp.arange(P_SIZE, dtype=jnp.float32) - (P_SIZE - 1) / 2.0
    tilt = (
        coord[None, :, None] * coords_xy[0][None, None, :]
        + coord[:, None, None] * coords_xy[1][None, None, :]
    )
    wide = group * count
    phases_wide = phases[:, :, None, :].reshape(P_SIZE, P_SIZE, wide)
    tilt_wide = tilt[:, :, None, :].reshape(P_SIZE, P_SIZE, wide)
    ampl_wide = ampl[:, :, None, :].reshape(P_SIZE, P_SIZE, wide)
    dens_blocks = densities.reshape(blocks, group)
    weight_blocks = weights.reshape(blocks, group)

    def step(accum, block):
        offsets = block * group + jnp.arange(group, dtype=jnp.int32)
        global_bin = first_bin + offsets
        kappa = ELONG * (2.0 * global_bin.astype(jnp.float32) / (nbins_all - 1) - 1.0)
        kappa_wide = jnp.broadcast_to(kappa[:, None], (group, count)).reshape(wide)
        psi = phases_wide + kappa_wide[None, None, :] * tilt_wide
        intensity, pull = jax.vjp(
            lambda value: spot_image(value, ampl_wide, table_re, table_im, P_SIZE), psi
        )
        scale = dens_blocks[block] * weight_blocks[block]
        seed = (grad_img[:, :, None, :] * scale[None, None, :, None]).reshape(FIELD, FIELD, wide)
        (dpsi,) = pull(seed)
        stat = jnp.sum(
            grad_img[:, :, None, :] * intensity.reshape(FIELD, FIELD, group, count), axis=(0, 1, 3)
        )
        return (accum + jnp.sum(dpsi.reshape(P_SIZE, P_SIZE, group, count), axis=2), stat)

    accum, stats = lax.scan(
        step, jnp.zeros((P_SIZE, P_SIZE, count), jnp.float32), jnp.arange(blocks, dtype=jnp.int32)
    )
    return (accum.reshape(P_SIZE * P_SIZE, count), stats.reshape(total_bins))


def local(cotangent, amplitude, phase, position, profile, alt_weight):
    n_alt = lax.axis_size("alt")
    nsub_all = lax.axis_size("sub") * phase.shape[1]
    local_bins = profile.shape[0]
    nbins_all = n_alt * local_bins
    first_bin = lax.axis_index("alt") * local_bins
    grad_rows, ampl_rows = (
        lax.all_gather(cotangent, "alt", axis=0, tiled=True),
        lax.all_gather(amplitude, "alt", axis=0, tiled=True),
    )
    phase_rows = lax.all_gather(phase, "alt", axis=0, tiled=True)
    accum, stats = run_bins(
        grad_rows, ampl_rows, phase_rows, position, profile, alt_weight, first_bin, nbins_all, 1
    )
    partial_value = lax.psum_scatter(accum, "alt", scatter_dimension=0, tiled=True)
    total = lax.psum(jnp.sum(profile), "alt")
    mine = lax.psum(stats, "sub")
    centre = lax.psum(jnp.sum(profile * alt_weight * mine), "alt")
    phase_grad = partial_value / total
    profile_grad = (alt_weight * mine / total - centre / (total * total)) / nsub_all
    return (phase_grad, profile_grad)


def solution(mesh):
    placed = (P("alt", "sub"), P("alt", "sub"), P("alt", "sub"), P(None, "sub"), P("alt"), P("alt"))
    return jax.shard_map(
        local, mesh=mesh, in_specs=placed, out_specs=(P("alt", "sub"), P("alt")), check_vma=False
    )
```

profile of v0, /device:TPU:1, one launch (start us, length us, event | category | flops | bytes accessed | tf_op | source)
XLA Modules:
  0.0 271.2 jit_solution(8306988661547743573)
XLA Ops:
  8.0 19.8 %all_gather.10 = bf16[1024,128]{1,0:T(8,128)(2,1)S(1)} all-gather(bf16[128,128]{1,0:T(8,128)(2,1)} %param.9), channel_id=1, replica_groups=mesh['sub'=32,'alt'=8] {'alt'}, dimensions={0}, use_global_device_ids=true | all-gather | bytes 294912 | tf_op jit(solution)/shard_map/all_gather | solution.py:92
  28.7 17.3 %all_gather.9 = f32[1024,128]{1,0:T(8,128)S(1)} all-gather(f32[128,128]{1,0:T(8,128)} %param.10), channel_id=1, replica_groups=mesh['sub'=32,'alt'=8] {'alt'}, dimensions={0}, use_global_device_ids=true | all-gather | bytes 589824 | tf_op jit(solution)/shard_map/all_gather | solution.py:94
  47.9 113.0 %while.16 = (s32[]{:T(128)}, f32[32,32,128]{2,1,0:T(8,128)}, f32[2,1]{0,1:T(1,128)S(1)}, s32[]{:T(128)}, s32[2]{0:T(128)S(1)}, /*index=5*/f32[32,32,128]{2,1,0:T...) while((s32[]{:T(128)}, f32[32,32,128]{2,1,0:T(8,128)}, ...), condition=%wide.region_2.3_spmd.clone.clone, body=%wide.region_0.2_spmd.clone.clone.sunk | while | flops 2435006464 | bytes 95617512 | solution.py:78
  53.4 2.7 %fusion.224 = f32[32,128,64]{1,2,0:T(8,128)S(1)} fusion(f32[32,32,128]{2,1,0:T(8,128)S(1)} %get-tuple-element.460, f32[32,32,128]{2,1,0:T(8,128)S(1)} %get-tuple-element.459, f32[32,128]{1,0:T(8,128)S(1)} %get-tuple-element.464, f32[32,128]{1,0:T(8,128)S(1)} %get-tuple-element.465, f32[]{:T(128)} %bitcast.156), kind=kOutput, calls=%fused_computation.52.clone.1 | convolution fusion | flops 101216256 | bytes 2129924 | tf_op jit(solution)/shard_map/while/body/eval_jaxpr/jvp(kj,ajs->aks)/dot_general | solution.py:27
  56.2 2.7 %fusion.225 = f32[32,64,128]{2,1,0:T(8,128)S(1)} fusion(f32[32,128,64]{1,2,0:T(8,128)S(1)} %fusion.224, f32[32,32,128]{2,1,0:T(8,128)S(1)} %get-tuple-element.460, f32[32,32,128]{2,1,0:T(8,128)S(1)} %get-tuple-element.459, f32[32,128]{1,0:T(8,128)S(1)} %get-tuple-element.464, f32[32,128]{1,0:T(8,128)S(1)} %get-tuple-element.465, f32[]{:T(128)} %bitcast.156), kind=kOutput, calls=%fused_computation.19.clone.1 | convolution fusion | flops 101480448 | bytes 3178500 | tf_op jit(solution)/shard_map/while/body/eval_jaxpr/jvp(kj,ajs->aks)/dot_general | solution.py:27
  58.9 2.7 %fusion.221 = f32[32,128,64]{1,2,0:T(8,128)S(1)} fusion(f32[32,32,128]{2,1,0:T(8,128)S(1)} %get-tuple-element.460, f32[32,32,128]{2,1,0:T(8,128)S(1)} %get-tuple-element.459, f32[32,128]{1,0:T(8,128)S(1)} %get-tuple-element.464, f32[32,128]{1,0:T(8,128)S(1)} %get-tuple-element.465, f32[]{:T(128)} %bitcast.156), kind=kOutput, calls=%fused_computation.51.clone.1 | convolution fusion | flops 101216256 | bytes 2129924 | tf_op jit(solution)/shard_map/while/body/eval_jaxpr/jvp(kj,ajs->aks)/dot_general | solution.py:24
  61.6 2.8 %fusion.222 = f32[32,64,128]{2,1,0:T(8,128)S(1)} fusion(f32[32,128,64]{1,2,0:T(8,128)S(1)} %fusion.221, f32[32,32,128]{2,1,0:T(8,128)S(1)} %get-tuple-element.460, f32[32,32,128]{2,1,0:T(8,128)S(1)} %get-tuple-element.459, f32[32,128]{1,0:T(8,128)S(1)} %get-tuple-element.464, f32[32,128]{1,0:T(8,128)S(1)} %get-tuple-element.465, f32[]{:T(128)} %bitcast.156), kind=kOutput, calls=%fused_computation.17.clone.1 | convolution fusion | flops 101480448 | bytes 3178500 | tf_op jit(solution)/shard_map/while/body/eval_jaxpr/jvp(kj,ajs->aks)/dot_general | solution.py:24
  64.4 2.7 fusion.223
  67.1 2.6 convolution_subtract_fusion.3
  72.2 5.7 %fusion.227 = (f32[]{:T(128)}, f32[64,128,64]{1,2,0:T(8,128)}) fusion(f32[64,128,64]{1,2,0:T(8,128)S(1)} %convolution_subtract_fusion.3, f32[64,64,128]{2,1,0:T(8,128)S(1)} %bitcast.161, f32[64,128,64]{1,2,0:T(8,128)S(1)} %fusion.226, f32[32,64,128]{2,1,0:T(8,128)S(1)} %fusion.222), kind=kOutput, calls=%fused_computation.4.clone.1 | convolution fusion | flops 205027328 | bytes 9437188 | tf_op jit(solution)/shard_map/while/body/eval_jaxpr/jvp(ka,ams->kms)/dot_general | solution.py:33
  78.8 5.0 %fusion.232 = f32[64,128,32]{1,2,0:T(8,128)S(1)} fusion(f32[64,128,64]{1,2,0:T(8,128)} %get-tuple-element.414, f32[64,64,128]{2,1,0:T(8,128)S(1)} %bitcast.162, f32[]{:T(128)} %bitcast.159), kind=kOutput, calls=%fused_computation.47.clone.1 | convolution fusion | flops 203454464 | bytes 5242884 | tf_op jit(solution)/shard_map/while/body/eval_jaxpr/transpose(jvp(ka,ams->kms))/dot_general | solution.py:33
  83.8 3.5 %fusion.229 = f32[64,128,32]{1,2,0:T(8,128)S(1)} fusion(f32[64,128,64]{1,2,0:T(8,128)S(1)} %copy-done.2, f32[64,64,128]{2,1,0:T(8,128)S(1)} %bitcast.163, f32[]{:T(128)} %bitcast.159), kind=kOutput, calls=%fused_computation.48.clone.1 | convolution fusion | flops 203452416 | bytes 5242884 | tf_op jit(solution)/shard_map/while/body/eval_jaxpr/transpose(jvp(ka,ams->kms))/dot_general | solution.py:33
  87.3 3.3 %fusion.230 = f32[32,128,64]{1,0,2:T(8,128)S(1)} fusion(f32[64,128,32]{1,2,0:T(8,128)S(1)} %fusion.229, f32[64,128,64]{1,2,0:T(8,128)S(1)} %copy-done.1, f32[64,64,128]{2,1,0:T(8,128)S(1)} %bitcast.164, f32[]{:T(128)} %bitcast.159), kind=kOutput, calls=%fused_computation.13.clone.1 | convolution fusion | flops 204240896 | bytes 6291460 | tf_op jit(solution)/shard_map/while/body/eval_jaxpr/transpose(jvp(ka,ams->kms))/dot_general | solution.py:30
  90.6 3.4 %fusion.233 = (f32[32,128,64]{1,0,2:T(8,128)S(1)}, f32[32,128,64]{1,0,2:T(8,128)S(1)}) fusion(f32[64,128,32]{1,2,0:T(8,128)S(1)} %fusion.232, f32[64,128,64]{1,2,0:T(8,128)S(1)} %copy-done.1, f32[64,64,128]{2,1,0:T(8,128)S(1)} %bitcast.165, f32[]{:T(128)} %bitcast.159), kind=kOutput, calls=%fused_computation.159.clone.1 | convolution fusion | flops 203976704 | bytes 7340036 | tf_op jit(solution)/shard_map/while/body/eval_jaxpr/transpose(jvp(ka,ams->kms))/dot_general | solution.py:30
  97.1 3.0 %fusion.234 = f32[32,32,128]{2,1,0:T(8,128)S(1)} fusion(f32[32,32,128]{2,1,0:T(8,128)S(1)} %get-tuple-element.460, f32[32,128,32]{1,2,0:T(8,128)S(1)} %fusion.231, f32[32,128,64]{1,0,2:T(8,128)S(1)} %get-tuple-element.415, f32[32,32,128]{2,1,0:T(8,128)S(1)} %get-tuple-element.459, f32[32,128]{1,0:T(8,128)S(1)} %get-tuple-element.464, ...), kind=kOutput, calls=%fused_computation.24.clone.1 | convolution fusion | flops 101609472 | bytes 3178500 | tf_op jit(solution)/shard_map/while/body/eval_jaxpr/transpose(jvp(kj,ajs->aks))/dot_general | solution.py:24
  100.1 3.0 %fusion.236 = f32[32,32,128]{2,1,0:T(8,128)S(1)} fusion(f32[32,32,128]{2,1,0:T(8,128)S(1)} %fusion.234, f32[32,32,128]{2,1,0:T(8,128)S(1)} %get-tuple-element.460, f32[32,128,32]{1,2,0:T(8,128)S(1)} %fusion.235, f32[32,128,64]{1,0,2:T(8,128)S(1)} %get-tuple-element.416, f32[32,32,128]{2,1,0:T(8,128)S(1)} %copy-done.3, ...), kind=kOutput, calls=%fused_computation.30.clone.1 | convolution fusion | flops 101873664 | bytes 4227077 | tf_op jit(solution)/shard_map/while/body/eval_jaxpr/transpose(jvp(kj,ajs->aks))/dot_general | solution.py:24
  109.1 2.7 %fusion.224 = f32[32,128,64]{1,2,0:T(8,128)S(1)} fusion(f32[32,32,128]{2,1,0:T(8,128)S(1)} %get-tuple-element.460, f32[32,32,128]{2,1,0:T(8,128)S(1)} %get-tuple-element.459, f32[32,128]{1,0:T(8,128)S(1)} %get-tuple-element.464, f32[32,128]{1,0:T(8,128)S(1)} %get-tuple-element.465, f32[]{:T(128)} %bitcast.156), kind=kOutput, calls=%fused_computation.52.clone.1 | convolution fusion | flops 101216256 | bytes 2129924 | tf_op jit(solution)/shard_map/while/body/eval_jaxpr/jvp(kj,ajs->aks)/dot_general | solution.py:27
  111.9 2.7 %fusion.225 = f32[32,64,128]{2,1,0:T(8,128)S(1)} fusion(f32[32,128,64]{1,2,0:T(8,128)S(1)} %fusion.224, f32[32,32,128]{2,1,0:T(8,128)S(1)} %get-tuple-element.460, f32[32,32,128]{2,1,0:T(8,128)S(1)} %get-tuple-element.459, f32[32,128]{1,0:T(8,128)S(1)} %get-tuple-element.464, f32[32,128]{1,0:T(8,128)S(1)} %get-tuple-element.465, f32[]{:T(128)} %bitcast.156), kind=kOutput, calls=%fused_computation.19.clone.1 | convolution fusion | flops 101480448 | bytes 3178500 | tf_op jit(solution)/shard_map/while/body/eval_jaxpr/jvp(kj,ajs->aks)/dot_general | solution.py:27
  114.6 2.7 %fusion.221 = f32[32,128,64]{1,2,0:T(8,128)S(1)} fusion(f32[32,32,128]{2,1,0:T(8,128)S(1)} %get-tuple-element.460, f32[32,32,128]{2,1,0:T(8,128)S(1)} %get-tuple-element.459, f32[32,128]{1,0:T(8,128)S(1)} %get-tuple-element.464, f32[32,128]{1,0:T(8,128)S(1)} %get-tuple-element.465, f32[]{:T(128)} %bitcast.156), kind=kOutput, calls=%fused_computation.51.clone.1 | convolution fusion | flops 101216256 | bytes 2129924 | tf_op jit(solution)/shard_map/while/body/eval_jaxpr/jvp(kj,ajs->aks)/dot_general | solution.py:24
  117.3 2.8 %fusion.222 = f32[32,64,128]{2,1,0:T(8,128)S(1)} fusion(f32[32,128,64]{1,2,0:T(8,128)S(1)} %fusion.221, f32[32,32,128]{2,1,0:T(8,128)S(1)} %get-tuple-element.460, f32[32,32,128]{2,1,0:T(8,128)S(1)} %get-tuple-element.459, f32[32,128]{1,0:T(8,128)S(1)} %get-tuple-element.464, f32[32,128]{1,0:T(8,128)S(1)} %get-tuple-element.465, f32[]{:T(128)} %bitcast.156), kind=kOutput, calls=%fused_computation.17.clone.1 | convolution fusion | flops 101480448 | bytes 3178500 | tf_op jit(solution)/shard_map/while/body/eval_jaxpr/jvp(kj,ajs->aks)/dot_general | solution.py:24
  120.1 2.7 %fusion.223 = f32[64,128,64]{1,2,0:T(8,128)S(1)} fusion(f32[32,64,128]{2,1,0:T(8,128)S(1)} %fusion.222), kind=kOutput, calls=%fused_computation.37.clone.1 | convolution fusion | flops 201355264 | bytes 3145728 | tf_op jit(solution)/shard_map/while/body/eval_jaxpr/jvp(ka,ams->kms)/dot_general | solution.py:30
  122.8 2.6 convolution_subtract_fusion.3
  125.4 2.5 fusion.226
  128.0 5.7 %fusion.227 = (f32[]{:T(128)}, f32[64,128,64]{1,2,0:T(8,128)}) fusion(f32[64,128,64]{1,2,0:T(8,128)S(1)} %convolution_subtract_fusion.3, f32[64,64,128]{2,1,0:T(8,128)S(1)} %bitcast.161, f32[64,128,64]{1,2,0:T(8,128)S(1)} %fusion.226, f32[32,64,128]{2,1,0:T(8,128)S(1)} %fusion.222), kind=kOutput, calls=%fused_computation.4.clone.1 | convolution fusion | flops 205027328 | bytes 9437188 | tf_op jit(solution)/shard_map/while/body/eval_jaxpr/jvp(ka,ams->kms)/dot_general | solution.py:33
  134.8 5.0 %fusion.232 = f32[64,128,32]{1,2,0:T(8,128)S(1)} fusion(f32[64,128,64]{1,2,0:T(8,128)} %get-tuple-element.414, f32[64,64,128]{2,1,0:T(8,128)S(1)} %bitcast.162, f32[]{:T(128)} %bitcast.159), kind=kOutput, calls=%fused_computation.47.clone.1 | convolution fusion | flops 203454464 | bytes 5242884 | tf_op jit(solution)/shard_map/while/body/eval_jaxpr/transpose(jvp(ka,ams->kms))/dot_general | solution.py:33
  139.8 3.5 %fusion.229 = f32[64,128,32]{1,2,0:T(8,128)S(1)} fusion(f32[64,128,64]{1,2,0:T(8,128)S(1)} %copy-done.2, f32[64,64,128]{2,1,0:T(8,128)S(1)} %bitcast.163, f32[]{:T(128)} %bitcast.159), kind=kOutput, calls=%fused_computation.48.clone.1 | convolution fusion | flops 203452416 | bytes 5242884 | tf_op jit(solution)/shard_map/while/body/eval_jaxpr/transpose(jvp(ka,ams->kms))/dot_general | solution.py:33
  143.3 3.3 %fusion.230 = f32[32,128,64]{1,0,2:T(8,128)S(1)} fusion(f32[64,128,32]{1,2,0:T(8,128)S(1)} %fusion.229, f32[64,128,64]{1,2,0:T(8,128)S(1)} %copy-done.1, f32[64,64,128]{2,1,0:T(8,128)S(1)} %bitcast.164, f32[]{:T(128)} %bitcast.159), kind=kOutput, calls=%fused_computation.13.clone.1 | convolution fusion | flops 204240896 | bytes 6291460 | tf_op jit(solution)/shard_map/while/body/eval_jaxpr/transpose(jvp(ka,ams->kms))/dot_general | solution.py:30
  146.6 3.4 %fusion.233 = (f32[32,128,64]{1,0,2:T(8,128)S(1)}, f32[32,128,64]{1,0,2:T(8,128)S(1)}) fusion(f32[64,128,32]{1,2,0:T(8,128)S(1)} %fusion.232, f32[64,128,64]{1,2,0:T(8,128)S(1)} %copy-done.1, f32[64,64,128]{2,1,0:T(8,128)S(1)} %bitcast.165, f32[]{:T(128)} %bitcast.159), kind=kOutput, calls=%fused_computation.159.clone.1 | convolution fusion | flops 203976704 | bytes 7340036 | tf_op jit(solution)/shard_map/while/body/eval_jaxpr/transpose(jvp(ka,ams->kms))/dot_general | solution.py:30
  152.8 3.0 %fusion.234 = f32[32,32,128]{2,1,0:T(8,128)S(1)} fusion(f32[32,32,128]{2,1,0:T(8,128)S(1)} %get-tuple-element.460, f32[32,128,32]{1,2,0:T(8,128)S(1)} %fusion.231, f32[32,128,64]{1,0,2:T(8,128)S(1)} %get-tuple-element.415, f32[32,32,128]{2,1,0:T(8,128)S(1)} %get-tuple-element.459, f32[32,128]{1,0:T(8,128)S(1)} %get-tuple-element.464, ...), kind=kOutput, calls=%fused_computation.24.clone.1 | convolution fusion | flops 101609472 | bytes 3178500 | tf_op jit(solution)/shard_map/while/body/eval_jaxpr/transpose(jvp(kj,ajs->aks))/dot_general | solution.py:24
  155.8 3.0 %fusion.236 = f32[32,32,128]{2,1,0:T(8,128)S(1)} fusion(f32[32,32,128]{2,1,0:T(8,128)S(1)} %fusion.234, f32[32,32,128]{2,1,0:T(8,128)S(1)} %get-tuple-element.460, f32[32,128,32]{1,2,0:T(8,128)S(1)} %fusion.235, f32[32,128,64]{1,0,2:T(8,128)S(1)} %get-tuple-element.416, f32[32,32,128]{2,1,0:T(8,128)S(1)} %copy-done.3, ...), kind=kOutput, calls=%fused_computation.30.clone.1 | convolution fusion | flops 101873664 | bytes 4227077 | tf_op jit(solution)/shard_map/while/body/eval_jaxpr/transpose(jvp(kj,ajs->aks))/dot_general | solution.py:24
  161.0 68.7 %psum.22 = f32[2]{0:T(128)S(1)} all-reduce(f32[2]{0:T(128)S(1)} %bitcast.174), channel_id=1, replica_groups=mesh['sub'=32,'alt'=8] {'sub'}, use_global_device_ids=true, to_apply=%region_6.7 | all-reduce | flops 2 | bytes 16 | tf_op jit(solution)/shard_map/psum | solution.py:100
  230.3 28.4 %all-reduce = (f32[]{:T(128)}, f32[]{:T(128)}) all-reduce(f32[]{:T(128)} %get-tuple-element.302, f32[]{:T(128)} %get-tuple-element.301), channel_id=1, replica_groups=mesh['sub'=32,'alt'=8] {'alt'}, use_global_device_ids=true, to_apply=%region_5.6 | all-reduce | flops 2 | bytes 16 | tf_op jit(solution)/shard_map/psum | solution.py:99
  (54 shorter events, 24.5 us)
Async XLA Ops:
  7.2 39.4 %all-gather.2.cloned.1.call-start = ((), (), s32[]{:S(2)}) async-start(), calls=%async_computation.1 | async-start | bytes 1179648 | tf_op jit(solution)/shard_map/all_gather | solution.py:91
  7.9 254.0 %reduce-scatter.2.cloned.1.call-start = ((), (), s32[]{:S(2)}) async-start(), calls=%async_computation.2 | async-start | bytes 589824 | tf_op jit(solution)/shard_map/reduce_scatter | solution.py:98
  27.8 20.2 %copy-start.5 = (f32[2]{0:T(128)S(1)}, f32[2]{0:T(128)}, u32[]{:S(2)}) copy-start(f32[2]{0:T(128)} %param.12) | copy-start | bytes 28
  27.8 20.2 %copy-start.6 = (f32[2]{0:T(128)S(1)}, f32[2]{0:T(128)}, u32[]{:S(2)}) copy-start(f32[2]{0:T(128)} %param.13) | copy-start | bytes 28
  69.7 8.2 %copy-start = (f32[64,128,64]{1,2,0:T(8,128)}, f32[64,128,64]{1,2,0:T(8,128)S(1)}, u32[]{:S(2)}) copy-start(f32[64,128,64]{1,2,0:T(8,128)S(1)} %convolution_subtract_fusion.3) | copy-start | bytes 6291460 | tf_op jit(solution)/shard_map/while
  78.8 5.0 %copy-start.2 = (f32[64,128,64]{1,2,0:T(8,128)S(1)}, f32[64,128,64]{1,2,0:T(8,128)}, u32[]{:S(2)}) copy-start(f32[64,128,64]{1,2,0:T(8,128)} %get-tuple-element.414) | copy-start | bytes 6291460 | tf_op jit(solution)/shard_map/while
  83.8 3.5 %copy-start.1 = (f32[64,128,64]{1,2,0:T(8,128)S(1)}, f32[64,128,64]{1,2,0:T(8,128)}, u32[]{:S(2)}) copy-start(f32[64,128,64]{1,2,0:T(8,128)} %copy-done) | copy-start | bytes 6291460 | tf_op jit(solution)/shard_map/while
  95.7 4.3 %copy-start.3 = (f32[32,32,128]{2,1,0:T(8,128)S(1)}, f32[32,32,128]{2,1,0:T(8,128)}, u32[]{:S(2)}) copy-start(f32[32,32,128]{2,1,0:T(8,128)} %get-tuple-element.437) | copy-start | bytes 1572868 | tf_op jit(solution)/shard_map/while
  103.1 0.8 copy-start.4
  125.4 8.2 %copy-start = (f32[64,128,64]{1,2,0:T(8,128)}, f32[64,128,64]{1,2,0:T(8,128)S(1)}, u32[]{:S(2)}) copy-start(f32[64,128,64]{1,2,0:T(8,128)S(1)} %convolution_subtract_fusion.3) | copy-start | bytes 6291460 | tf_op jit(solution)/shard_map/while
  134.8 5.0 %copy-start.2 = (f32[64,128,64]{1,2,0:T(8,128)S(1)}, f32[64,128,64]{1,2,0:T(8,128)}, u32[]{:S(2)}) copy-start(f32[64,128,64]{1,2,0:T(8,128)} %get-tuple-element.414) | copy-start | bytes 6291460 | tf_op jit(solution)/shard_map/while
  139.8 3.5 %copy-start.1 = (f32[64,128,64]{1,2,0:T(8,128)S(1)}, f32[64,128,64]{1,2,0:T(8,128)}, u32[]{:S(2)}) copy-start(f32[64,128,64]{1,2,0:T(8,128)} %copy-done) | copy-start | bytes 6291460 | tf_op jit(solution)/shard_map/while
  151.5 4.3 %copy-start.3 = (f32[32,32,128]{2,1,0:T(8,128)S(1)}, f32[32,32,128]{2,1,0:T(8,128)}, u32[]{:S(2)}) copy-start(f32[32,32,128]{2,1,0:T(8,128)} %get-tuple-element.437) | copy-start | bytes 1572868 | tf_op jit(solution)/shard_map/while
  158.8 0.8 copy-start.4
Sparse Core Ops, SparseCore 0:
  9.8 36.6 all-gather.1
  161.1 35.4 reduce-scatter.1
where the time goes:
time: 274 us; the launch traced here: 271 us
  blocking collectives  134 us (49%)
  matrix products  97 us (35%)
  between operations  16.4 us (6%)
  other arithmetic  7.92 us (3%)
  loops' own time  7.44 us (3%)
  local copies, waits for them, and re-layouts  6.87 us (3%)
    psum x1, blocking collectives, local(): mine = lax.psum(stats, 'sub')  68.7 us
    psum x1, blocking collectives, local(): total = lax.psum(jnp.sum(profile), 'alt')  28.4 us
    dot_general x4, matrix products, spot_image(): jnp.einsum('ka,ams->kms', table_im, first_re, precision=high)  21.3 us
    all_gather x1, blocking collectives, local(): lax.all_gather(amplitude, 'alt', axis=0, tiled=True)  19.8 us
    all_gather x1, blocking collectives, local(): phase_rows = lax.all_gather(phase, 'alt', axis=0, tiled=True)  17.3 us
    dot_general x4, matrix products, spot_image(): jnp.einsum('ka,ams->kms', table_re, first_re, precision=high)  12.1 us
    dot_general x4, matrix products, spot_image(): jnp.einsum('ka,ams->kms', table_re, first_im, precision=high)  12 us
    dot_general x4, matrix products, spot_image(): jnp.einsum('ka,ams->kms', table_im, first_im, precision=high)  11.8 us
  transfers between devices with their start and end apart: 2, of which 1 were waited for; matrix products, arithmetic and copies ran while one was open for 1% of the time, Pallas kernels for 0%

commit v1 on v0

v1 whole, which is shorter than its diff:
```python
import functools

import jax
import jax.numpy as jnp
import numpy as np
from jax import lax
from jax.experimental import pallas as pl
from jax.experimental.pallas import tpu as pltpu
from jax.sharding import PartitionSpec as P

F32 = jnp.float32
BF16 = jnp.bfloat16
MESH = pl.DeviceIdType.MESH

N_PUPIL = 32
N_FIELD = 64
N_BINS = 16
N_ALT = 8
LANES = 128


def split_np(m):
    hi = np.asarray(m, np.float32).astype(BF16)
    lo = (np.asarray(m, np.float64) - hi.astype(np.float64)).astype(np.float32).astype(BF16)
    return hi, lo


def make_tables():
    n = np.arange(N_FIELD)
    angle = 2.0 * np.pi / N_FIELD * (np.outer(n, n) % N_FIELD)
    cos, sin = np.cos(angle), np.sin(angle)
    eye = np.eye(4)
    half_c, half_s = cos[:, :N_PUPIL], sin[:, :N_PUPIL]
    kc, ks = np.kron(eye, half_c), np.kron(eye, half_s)
    w1 = np.block([[kc.T, -ks.T], [ks.T, kc.T]])
    w3 = np.block([[kc, ks]])
    w4 = w3.T
    w5 = np.block([[kc, ks], [-ks, kc]])
    a2 = np.block([[half_c, half_s], [-half_s, half_c]])
    a3 = np.vstack([cos, sin])
    a5 = np.block([[cos[:N_PUPIL], -sin[:N_PUPIL]], [sin[:N_PUPIL], cos[:N_PUPIL]]])
    out = []
    for w in (w1, w3, w4, w5):
        out += list(split_np(w))
    for a in (a2, a3, a5):
        hi, lo = split_np(a)
        out.append(np.concatenate([hi, hi, lo], axis=1))
    return out


def split(x):
    hi = x.astype(BF16)
    return hi, (x - hi.astype(F32)).astype(BF16)


def mm(a, b):
    return jnp.dot(a, b, preferred_element_type=F32)


def lane_mm(x, w_hi, w_lo):
    hi, lo = split(x)
    rows = x.shape[0]
    both = mm(jnp.concatenate([hi, lo], axis=0), w_hi)
    return both[:rows] + both[rows:] + mm(hi, w_lo)


def row_mm(table, x):
    hi, lo = split(x)
    return mm(table, jnp.concatenate([hi, lo, hi], axis=0))


def sincos(x):
    n = jnp.floor(x * (2.0 / np.pi) + 0.5)
    r = x - n * 1.5703125
    r = r - n * 4.837512969970703125e-4
    r = r - n * 7.54978995489188216e-8
    z = r * r
    s = ((-1.9515295891e-4 * z + 8.3321608736e-3) * z - 1.6666654611e-1) * z * r + r
    c = ((2.443315711809948e-5 * z - 1.388731625493765e-3) * z + 4.166664568298827e-2) * z * z - 0.5 * z + 1.0
    q = n.astype(jnp.int32)
    odd = (q & 1) == 1
    sv = jnp.where(odd, c, s)
    cv = jnp.where(odd, s, c)
    sv = jnp.where((q & 2) == 2, -sv, sv)
    cv = jnp.where(((q + 1) & 2) == 2, -cv, cv)
    return sv, cv


def swap4(x):
    lane = lax.broadcasted_iota(jnp.int32, x[0].shape, 1)
    keep0 = ((lane // 4) % 2) == 0
    keep1 = ((lane // 8) % 2) == 0

    def pair(a, b, shift, keep):
        return (
            jnp.where(keep, a, pltpu.roll(b, shift, 1)),
            jnp.where(keep, pltpu.roll(a, LANES - shift, 1), b),
        )

    y0, y1 = pair(x[0], x[1], 4, keep0)
    y2, y3 = pair(x[2], x[3], 4, keep0)
    z0, z2 = pair(y0, y2, 8, keep1)
    z1, z3 = pair(y1, y3, 8, keep1)
    return z0, z1, z2, z3


def kernel(
    dims,
    cot_hbm, amp_hbm, ph_hbm, pos_ref, prof_ref, wt_ref,
    w1h_hbm, w1l_hbm, w3h_hbm, w3l_hbm, w4h_hbm, w4l_hbm, w5h_hbm, w5l_hbm, a2_hbm, a3_hbm, a5_hbm,
    out_ref, pg_ref,
    cot_in, amp_in, ph_in,
    w1h, w1l, w3h, w3l, w4h, w4l, w5h, w5l, a2, a3, a5,
    cot_send, amp_send, ph_send, small_send,
    cot_recv, amp_recv, ph_recv, small_recv,
    back_send, back_recv, st_a, st_b, row_a, row_b,
    yu, uf, bw, yg, cs, gf, qf, ct, sn, er, ei, sf,
    load_sem, send_sem, recv_sem, sa_send, sa_recv, sb_send, sb_recv,
):
    ny, nz, nx = dims
    me = lax.axis_index("alt")
    sub = lax.axis_index("sub")
    y, zl, x = sub // (nz * nx), (sub // nx) % nz, sub % nx

    plane = []
    for oy in range(ny):
        for ox in range(nx):
            if oy or ox:
                qy, qx = (y + oy) % ny, (x + ox) % nx
                plane.append(({"sub": qy * (nz * nx) + zl * nx + qx}, qy * nx + qx))
    column = []
    for oz in range(nz):
        for oa in range(N_ALT):
            if oz or oa:
                qz, qa = (zl + oz) % nz, (me + oa) % N_ALT
                column.append(({"sub": y * (nz * nx) + qz * nx + x, "alt": qa}, qz * N_ALT + qa))
    my_plane = y * nx + x
    my_column = zl * N_ALT + me

    loads = []
    for src, dst in (
        (ph_hbm, ph_in), (amp_hbm, amp_in), (cot_hbm, cot_in),
        (w1h_hbm, w1h), (w1l_hbm, w1l), (a2_hbm, a2), (w3h_hbm, w3h), (w3l_hbm, w3l), (a3_hbm, a3),
        (w4h_hbm, w4h), (w4l_hbm, w4l), (a5_hbm, a5), (w5h_hbm, w5h), (w5l_hbm, w5l),
    ):
        cp = pltpu.make_async_copy(src, dst, load_sem.at[len(loads)])
        cp.start()
        loads.append(cp)

    barrier = pltpu.get_barrier_semaphore()
    for device, _ in plane + column:
        pl.semaphore_signal(barrier, inc=1, device_id=device, device_id_type=MESH)

    row = lax.broadcasted_iota(jnp.int32, (8, LANES), 0)
    lane = lax.broadcasted_iota(jnp.int32, (8, LANES), 1)
    small = jnp.zeros((8, LANES), F32)
    for b in range(2):
        here = lane == 2 * me + b
        small = jnp.where(here & (row == 0), prof_ref[b], small)
        small = jnp.where(here & (row == 1), wt_ref[b], small)
    small_send[...] = small

    loads[0].wait()
    t = jnp.concatenate(swap4([ph_in[32 * k : 32 * k + 32, :] for k in range(4)]), axis=0).T
    ph_send[...] = t.reshape(8, 16, LANES)
    loads[1].wait()
    amp = amp_in[...].astype(F32)
    t = jnp.concatenate(swap4([amp[32 * k : 32 * k + 32, :] for k in range(4)]), axis=0).T
    amp_send[...] = t.reshape(8, 16, LANES).astype(BF16)

    pl.semaphore_wait(barrier, len(plane) + len(column))

    order = [4, 5, 2, 6, 3, 7, 1]
    kinds = ((small_send, small_recv), (ph_send, ph_recv), (amp_send, amp_recv), (cot_send, cot_recv), (back_send, back_recv))

    def exchange(kind, offset):
        src, dst = kinds[kind]
        peer = (me + offset) % N_ALT
        return pltpu.make_async_remote_copy(
            src_ref=src if kind == 0 else src.at[peer],
            dst_ref=dst.at[me],
            send_sem=send_sem.at[kind, peer],
            recv_sem=recv_sem.at[kind, me],
            device_id={"alt": peer},
            device_id_type=MESH,
        )

    def arrival(kind, offset):
        src, dst = kinds[kind]
        peer = (me + offset) % N_ALT
        return pltpu.make_async_remote_copy(
            src_ref=src if kind == 0 else src.at[peer],
            dst_ref=dst.at[peer],
            send_sem=send_sem.at[kind, peer],
            recv_sem=recv_sem.at[kind, peer],
            device_id={"alt": peer},
            device_id_type=MESH,
        )

    def start(kind):
        for offset in order:
            exchange(kind, offset).start()

    def wait_in(kind):
        for offset in order:
            arrival(kind, offset).wait_recv()

    def wait_out(kind):
        for offset in order:
            exchange(kind, offset).wait_send()

    start(0)
    start(1)
    start(2)

    loads[2].wait()
    for half in range(2):
        z = swap4([cot_in[256 * half + 64 * k : 256 * half + 64 * k + 64, :].astype(F32) for k in range(4)])
        for u in range(2):
            t = jnp.concatenate([z[2 * u], z[2 * u + 1]], axis=0).T
            cot_send[:, 16 * half : 16 * half + 16, LANES * u : LANES * u + LANES] = t.reshape(8, 16, LANES).astype(BF16)
    start(3)

    small_recv[me] = small
    ph_recv[me] = ph_send[me]
    amp_recv[me] = amp_send[me]
    cot_recv[me] = cot_send[me]

    src = lax.broadcasted_iota(jnp.int32, (LANES, 4 * LANES), 0)
    dst = lax.broadcasted_iota(jnp.int32, (LANES, 4 * LANES), 1)
    pick = (src == 16 * me + 4 * ((dst % LANES) // 32) + dst // LANES).astype(F32)
    pos = jnp.concatenate([pos_ref[...], jnp.zeros((6, LANES), F32)], axis=0)
    pos = jnp.dot(pos, pick, precision=lax.Precision.HIGHEST, preferred_element_type=F32)
    r64 = lax.broadcasted_iota(jnp.int32, (N_FIELD, LANES), 0)
    l64 = lax.broadcasted_iota(jnp.int32, (N_FIELD, LANES), 1)
    dr = jnp.where(r64 < 32, r64, r64 - N_FIELD).astype(F32)
    dc = (l64 % 32).astype(F32)
    twice = jnp.where(l64 % 32 == 0, 1.0, 2.0).astype(F32)
    for g in range(4):
        px = pos[0:1, LANES * g : LANES * g + LANES]
        py = pos[1:2, LANES * g : LANES * g + LANES]
        s, c = sincos(0.05 * (px * dc + py * dr))
        c2, s2 = c * c - s * s, 2.0 * s * c
        for j in range(8):
            ct[j, g], sn[j, g] = c, s
            if j < 7:
                c, s = c * c2 - s * s2, s * c2 + c * s2

    wait_in(0)
    bins = small_recv[0]
    for k in range(1, N_ALT):
        bins = bins + small_recv[k]
    prof, wt = bins[0:1, :], bins[1:2, :]
    total = jnp.sum(prof, axis=1, keepdims=True)
    omega = prof * wt / total
    for g in range(4):
        re = jnp.zeros((N_FIELD, LANES), F32)
        im = jnp.zeros((N_FIELD, LANES), F32)
        for j in range(8):
            up, down = omega[:, 8 + j : 9 + j], omega[:, 7 - j : 8 - j]
            re = re + (up + down) * ct[j, g]
            im = im - (up - down) * sn[j, g]
        sf[0, g] = re * twice
        sf[1, g] = im * twice

    for cp in loads[3:]:
        cp.wait()
    wait_in(1)
    wait_in(2)
    s, c = sincos(ph_recv[...].reshape(LANES, LANES))
    amp = amp_recv[...].astype(F32).reshape(LANES, LANES)
    e_re, e_im = amp * c, amp * s
    er[...] = e_re
    ei[...] = e_im
    yy = lane_mm(jnp.concatenate([e_re, e_im], axis=1), w1h[...], w1l[...])
    for k in range(4):
        yu[k] = yy[:, LANES * k : LANES * k + LANES]
    power = []
    for g in range(4):
        m = [yu.at[k][pl.ds(g, 32, stride=4), :] for k in range(4)]
        m = [jnp.concatenate([m[0], m[1]], axis=1), jnp.concatenate([m[2], m[3]], axis=1)]
        u = row_mm(a2[...], jnp.concatenate(m, axis=0))
        uf[g] = u
        power.append(u[:64] * u[:64] + u[64:] * u[64:])
    yb = lane_mm(jnp.concatenate(power, axis=0), w3h[...], w3l[...])
    keep = jnp.where(r64 == 32, 0.0, twice) * (1.0 / (1024.0 * 4096.0))
    for g in range(4):
        v = row_mm(a3[...], yb[64 * g : 64 * g + 64, :])
        bw[0, g] = (v[:64, :LANES] - v[64:, LANES:]) * keep
        bw[1, g] = (v[:64, LANES:] + v[64:, :LANES]) * keep

    wait_in(3)
    cot = cot_recv[...].reshape(256, 256)
    yy = mm(cot, w3h[...]) + mm(cot, w3l[...])
    yg[0], yg[1] = yy[:, :LANES], yy[:, LANES:]
    for g in range(4):
        m = [yg.at[k][pl.ds(g, 64, stride=4), :] for k in range(2)]
        v = row_mm(a3[...], jnp.concatenate(m, axis=1))
        g_re = v[:64, :LANES] - v[64:, LANES:]
        g_im = v[:64, LANES:] + v[64:, :LANES]
        b_re, b_im, s_re, s_im = bw[0, g], bw[1, g], sf[0, g], sf[1, g]
        qf[0, g] = g_re * b_re + g_im * b_im
        qf[1, g] = g_im * b_re - g_re * b_im
        gf[g] = jnp.concatenate([g_re * s_re - g_im * s_im, g_re * s_im + g_im * s_re], axis=1)

    sums = []
    for part, table in ((0, ct), (1, sn)):
        rows = []
        for j in range(8):
            acc = jnp.zeros((8, LANES), F32)
            for g in range(4):
                acc = acc + jnp.sum((qf[part, g] * table[j, g]).reshape(8, 8, LANES), axis=0)
            rows.append(jnp.sum(acc, axis=0, keepdims=True))
        sums.append(jnp.sum(jnp.concatenate(rows, axis=0), axis=1, keepdims=True))
    here = jnp.where(lane == 8 + row, sums[0] + sums[1], 0.0) + jnp.where(lane == 7 - row, sums[0] - sums[1], 0.0)
    mine = jnp.sum(here, axis=0, keepdims=True)
    row_a[...] = mine
    st_a[my_plane] = mine

    def plane_copy(device, slot, me_slot, src, dst, ss, rs):
        return pltpu.make_async_remote_copy(
            src_ref=src, dst_ref=dst.at[me_slot], send_sem=ss.at[slot], recv_sem=rs.at[me_slot],
            device_id=device, device_id_type=MESH,
        )

    def plane_arrival(device, slot, src, dst, ss, rs):
        return pltpu.make_async_remote_copy(
            src_ref=src, dst_ref=dst.at[slot], send_sem=ss.at[slot], recv_sem=rs.at[slot],
            device_id=device, device_id_type=MESH,
        )

    for device, slot in plane:
        plane_copy(device, slot, my_plane, row_a, st_a, sa_send, sa_recv).start()

    z = []
    for g in range(4):
        v = row_mm(a3[...], gf[g])
        z.append(jnp.concatenate([v[:64, :LANES] + v[64:, LANES:], v[:64, LANES:] - v[64:, :LANES]], axis=1))
    g_hat = lane_mm(jnp.concatenate(z, axis=0), w4h[...], w4l[...])
    for g in range(4):
        gh = g_hat[64 * g : 64 * g + 64, :]
        v = jnp.concatenate([uf[g, :64, :] * gh, uf[g, 64:, :] * gh], axis=0)
        v = row_mm(a5[...], v)
        for k in range(2):
            cs.at[k][pl.ds(g, 32, stride=4), :] = v[:32, LANES * k : LANES * k + LANES]
            cs.at[2 + k][pl.ds(g, 32, stride=4), :] = v[32:, LANES * k : LANES * k + LANES]
    conv = lane_mm(jnp.concatenate([cs[k] for k in range(4)], axis=1), w5h[...], w5l[...])
    grad = (er[...] * conv[:, LANES:] - ei[...] * conv[:, :LANES]) * (2.0 / (1024.0 * 4096.0))
    back_send[...] = grad.reshape(8, 16, LANES)
    start(4)
    back_recv[me] = back_send[me]

    for device, slot in plane:
        plane_arrival(device, slot, row_a, st_a, sa_send, sa_recv).wait_recv()
    acc = st_a[0]
    for k in range(1, ny * nx):
        acc = acc + st_a[k]
    row_b[...] = acc
    st_b[my_column] = acc
    for device, slot in column:
        plane_copy(device, slot, my_column, row_b, st_b, sb_send, sb_recv).start()

    wait_in(4)
    m = back_recv[...].reshape(LANES, LANES).T
    rows = swap4([m[32 * k : 32 * k + 32, :] for k in range(4)])
    for k in range(4):
        out_ref[32 * k : 32 * k + 32, :] = rows[k]

    for device, slot in column:
        plane_arrival(device, slot, row_b, st_b, sb_send, sb_recv).wait_recv()
    stat = st_b[0]
    for k in range(1, nz * N_ALT):
        stat = stat + st_b[k]
    centre = jnp.sum(prof * wt * stat, axis=1, keepdims=True)
    n_all = ny * nz * nx * LANES
    pg = (wt * stat / total - centre / (total * total)) * (1.0 / n_all)
    for b in range(2):
        pg_ref[b] = jnp.sum(jnp.where(lane[0:1] == 2 * me + b, pg, 0.0))

    for kind in range(5):
        wait_out(kind)
    for device, slot in plane:
        plane_copy(device, slot, my_plane, row_a, st_a, sa_send, sa_recv).wait_send()
    for device, slot in column:
        plane_copy(device, slot, my_column, row_b, st_b, sb_send, sb_recv).wait_send()


def local(dims, cotangent, amplitude, phase, position, profile, alt_weight):
    tables = make_tables()
    any_spec = pl.BlockSpec(memory_space=pl.ANY)
    vmem = pl.BlockSpec(memory_space=pltpu.VMEM)
    smem = pl.BlockSpec(memory_space=pltpu.SMEM)
    n_plane, n_column = dims[0] * dims[2], dims[1] * N_ALT
    table_scratch = [pltpu.VMEM(t.shape, BF16) for t in tables]
    dma = pltpu.SemaphoreType.DMA
    return pl.pallas_call(
        functools.partial(kernel, dims),
        out_shape=(jax.ShapeDtypeStruct((LANES, LANES), F32), jax.ShapeDtypeStruct((2,), F32)),
        in_specs=[any_spec] * 3 + [vmem, smem, smem] + [any_spec] * len(tables),
        out_specs=(vmem, smem),
        scratch_shapes=[
            pltpu.VMEM((512, LANES), BF16), pltpu.VMEM((LANES, LANES), BF16), pltpu.VMEM((LANES, LANES), F32),
            *table_scratch,
            pltpu.VMEM((8, 32, 256), BF16), pltpu.VMEM((8, 16, LANES), BF16), pltpu.VMEM((8, 16, LANES), F32), pltpu.VMEM((8, LANES), F32),
            pltpu.VMEM((8, 32, 256), BF16), pltpu.VMEM((8, 16, LANES), BF16), pltpu.VMEM((8, 16, LANES), F32), pltpu.VMEM((8, 8, LANES), F32),
            pltpu.VMEM((8, 16, LANES), F32), pltpu.VMEM((8, 16, LANES), F32),
            pltpu.VMEM((n_plane, 1, LANES), F32), pltpu.VMEM((n_column, 1, LANES), F32),
            pltpu.VMEM((1, LANES), F32), pltpu.VMEM((1, LANES), F32),
            pltpu.VMEM((4, LANES, LANES), F32), pltpu.VMEM((4, LANES, 256), F32), pltpu.VMEM((2, 4, 64, LANES), F32),
            pltpu.VMEM((2, 256, LANES), F32), pltpu.VMEM((4, LANES, LANES), F32), pltpu.VMEM((4, 64, 256), F32),
            pltpu.VMEM((2, 4, 64, LANES), F32),
            pltpu.VMEM((8, 4, 64, LANES), F32), pltpu.VMEM((8, 4, 64, LANES), F32),
            pltpu.VMEM((LANES, LANES), F32), pltpu.VMEM((LANES, LANES), F32),
            pltpu.VMEM((2, 4, 64, LANES), F32),
            dma((14,)), dma((5, 8)), dma((5, 8)), dma((n_plane,)), dma((n_plane,)), dma((n_column,)), dma((n_column,)),
        ],
        compiler_params=pltpu.CompilerParams(collective_id=0, has_side_effects=True),
    )(cotangent, amplitude, phase, position, profile, alt_weight, *[jnp.asarray(t) for t in tables])


def solution(mesh):
    dims = {32: (4, 2, 4), 2: (2, 1, 1)}[mesh.shape["sub"]]
    placed = (P("alt", "sub"), P("alt", "sub"), P("alt", "sub"), P(None, "sub"), P("alt"), P("alt"))
    return jax.shard_map(
        functools.partial(local, dims), mesh=mesh, in_specs=placed, out_specs=(P("alt", "sub"), P("alt")), check_vma=False
    )
```

time: 274 us -> 35.5 us (0.13)
  blocking collectives: 134 us -> 0 us
  matrix products: 97 us -> 0 us
  Pallas kernels: 0 us -> 32.7 us
  between operations: 16.4 us -> 0.65 us
  other arithmetic: 7.92 us -> 0 us
  loops' own time: 7.44 us -> 0 us
  local copies, waits for them, and re-layouts: 6.87 us -> 1.99 us
    psum x2 -> x0, blocking collectives: 97.1 us -> none  [the longest x1 68.7 us: local(): mine = lax.psum(stats, 'sub')]
    dot_general x32 -> x0, matrix products: 97 us -> none  [the longest x4 21.3 us: spot_image(): jnp.einsum('ka,ams->kms', table_im, first_re, precision=high)]
    all_gather x2 -> x0, blocking collectives: 37.1 us -> none  [the longest x1 19.8 us: local(): lax.all_gather(amplitude, 'alt', axis=0, tiled=True)]
    pallas_call x0 -> x1, Pallas kernels: none -> 32.7 us  [local(): pl.pallas_call(functools.partial(kernel, dims), out_shape=(jax.ShapeDtype...]
    another operation x1 -> x0, loops' own time: 7.44 us -> none  [run_bins(): lax.scan(step, jnp.zeros((P_SIZE, P_SIZE, count), jnp.float32), jnp.arang...]
    div x2 -> x0, other arithmetic: 3.38 us -> none  [the longest x1 2.17 us: local(): phase_grad = partial_value / total]
  transfers between devices with their start and end apart: 2 -> 0, of which waited for: 1 -> 0; matrix products, arithmetic and copies ran while one was open for 1% -> 0% of each run, Pallas kernels for 0% -> 0%
where the time goes in v1:
time: 35.5 us; the launch traced here: 35.3 us
  Pallas kernels  32.7 us (92%)
  local copies, waits for them, and re-layouts  1.99 us (6%)
  between operations  0.65 us (2%)
    pallas_call x1, Pallas kernels, local(): pl.pallas_call(functools.partial(kernel, dims), out_shape=(jax.ShapeDtype...  32.7 us
    unnamed x4, local copies, waits for them, and re-layouts  1.99 us

profile of v1, /device:TPU:1, one launch (start us, length us, event | category | flops | bytes accessed | tf_op | source)
XLA Modules:
  0.0 35.3 jit_solution(6028279926811097938)
XLA Ops:
  0.6 32.7 %shard_map.176 = (f32[128,128]{1,0:T(8,128)}, f32[2]{0:T(128)}) custom-call(bf16[512,128]{1,0:T(8,128)(2,1)} %cot_hbm.1, bf16[128,128]{1,0:T(8,128)(2,1)} %amp_hbm.1, f32[128,128]{1,0:T(8,128)} %ph_hbm.1, f32[2,128]{1,0:T(2,128)} %pos_ref.1, f32[2]{0:T(128)} %prof_ref.1, f32[2]{0:T(128)} %wt_ref.1, bf16[256,512]{1,0:T(8,128)(2,1)} %constant.22.clone.w1h_hbm, ...), custom_call_target="tpu_custom_call" | custom-call | tf_op jit(solution)/shard_map/pallas_call | solution.py:396
  33.3 0.0 copy-start
  33.3 1.5 %copy.21 = f32[128,128]{1,0:T(8,128)} copy(f32[128,128]{1,0:T(8,128)} %get-tuple-element.4) | data formatting | bytes 131072
  34.8 0.0 copy-done
  34.8 0.5 %copy.22 = f32[2]{0:T(128)} copy(f32[2]{0:T(128)S(1)} %copy-done) | data formatting | bytes 16
Async XLA Ops:
  33.3 1.5 %copy-start = (f32[2]{0:T(128)S(1)}, f32[2]{0:T(128)}, u32[]{:S(2)}) copy-start(f32[2]{0:T(128)} %get-tuple-element.5) | copy-start | bytes 28

commit v2 on v1

v2 whole, which is shorter than its diff:
```python
import functools

import jax
import jax.numpy as jnp
import numpy as np
from jax import lax
from jax.experimental import pallas as pl
from jax.experimental.pallas import tpu as pltpu
from jax.sharding import PartitionSpec as P

F32 = jnp.float32
BF16 = jnp.bfloat16
MESH = pl.DeviceIdType.MESH

N_PUPIL = 32
N_FIELD = 64
N_BINS = 16
N_ALT = 8
LANES = 128


def split_np(m):
    hi = np.asarray(m, np.float32).astype(BF16)
    lo = (np.asarray(m, np.float64) - hi.astype(np.float64)).astype(np.float32).astype(BF16)
    return hi, lo


def make_tables():
    n = np.arange(N_FIELD)
    angle = 2.0 * np.pi / N_FIELD * (np.outer(n, n) % N_FIELD)
    cos, sin = np.cos(angle), np.sin(angle)
    eye = np.eye(4)
    half_c, half_s = cos[:, :N_PUPIL], sin[:, :N_PUPIL]
    kc, ks = np.kron(eye, half_c), np.kron(eye, half_s)
    w1 = np.block([[kc.T, -ks.T], [ks.T, kc.T]])
    w3 = np.block([[kc, ks]])
    w4 = w3.T
    w5 = np.block([[kc, ks], [-ks, kc]])
    a2 = np.block([[half_c, half_s], [-half_s, half_c]])
    a3 = np.vstack([cos, sin])
    a5 = np.block([[cos[:N_PUPIL], -sin[:N_PUPIL]], [sin[:N_PUPIL], cos[:N_PUPIL]]])
    blocks = []
    for w in (w1[:, :256], w1[:, 256:], w3, w4, w5[:256], w5[256:]):
        blocks += list(split_np(w))
    for a in (a2, a3):
        hi, lo = split_np(a)
        blocks.append(np.concatenate([hi, hi, lo, np.zeros_like(lo)], axis=1))
    hi, lo = split_np(a5)
    blocks += [np.concatenate([hi, hi], axis=1), np.concatenate([lo, np.zeros_like(lo)], axis=1)]
    return np.concatenate(blocks, axis=0)


W1, W3, W4, W5 = (0, 512), 1024, 1536, (2048, 2560)
A2, A3, A5 = 3072, 3200, 3328


def split(x):
    hi = x.astype(BF16)
    return hi, (x - hi.astype(F32)).astype(BF16)


def mm(a, b):
    return jnp.dot(a, b, preferred_element_type=F32)


def lane_mm(parts, tab, row):
    rows = parts[0].shape[0]
    w_hi, w_lo = tab[row : row + 256, :], tab[row + 256 : row + 512, :]
    both = mm(jnp.concatenate(parts, axis=0), w_hi)
    return both[:rows] + both[rows:] + mm(parts[0], w_lo)


def row_mm(table, x):
    hi, lo = split(x)
    return mm(table, jnp.concatenate([hi, lo, hi], axis=0))


def sincos(x):
    n = jnp.floor(x * (2.0 / np.pi) + 0.5)
    r = x - n * 1.5703125
    r = r - n * 4.837512969970703125e-4
    r = r - n * 7.54978995489188216e-8
    z = r * r
    s = ((-1.9515295891e-4 * z + 8.3321608736e-3) * z - 1.6666654611e-1) * z * r + r
    c = ((2.443315711809948e-5 * z - 1.388731625493765e-3) * z + 4.166664568298827e-2) * z * z - 0.5 * z + 1.0
    q = n.astype(jnp.int32)
    odd = (q & 1) == 1
    sv = jnp.where(odd, c, s)
    cv = jnp.where(odd, s, c)
    sv = jnp.where((q & 2) == 2, -sv, sv)
    cv = jnp.where(((q + 1) & 2) == 2, -cv, cv)
    return sv, cv


def swap4(x):
    lane = lax.broadcasted_iota(jnp.int32, x[0].shape, 1)
    keep0 = ((lane // 4) % 2) == 0
    keep1 = ((lane // 8) % 2) == 0

    def pair(a, b, shift, keep):
        return (
            jnp.where(keep, a, pltpu.roll(b, shift, 1)),
            jnp.where(keep, pltpu.roll(a, LANES - shift, 1), b),
        )

    y0, y1 = pair(x[0], x[1], 4, keep0)
    y2, y3 = pair(x[2], x[3], 4, keep0)
    z0, z2 = pair(y0, y2, 8, keep1)
    z1, z3 = pair(y1, y3, 8, keep1)
    return z0, z1, z2, z3


def kernel(
    dims,
    cot_hbm, amp_hbm, ph_hbm, pos_hbm, prof_hbm, wt_hbm,
    tab_hbm,
    grad_ref, bins_ref,
    cot_in, amp_in, ph_in, pos_ref,
    tab, prof_ref, wt_ref,
    cot_send, amp_send, ph_send, small_send,
    cot_recv, amp_recv, ph_recv, small_recv,
    back_send, back_recv, st_a, st_b, row_a, row_b,
    yu, uf, bw, yg, cs, gf, qf, ct, sn, er, ei, sf,
    load_sem, send_sem, recv_sem, sems_a, sems_b,
):
    ny, nz, nx = dims
    me = lax.axis_index("alt")
    sub = lax.axis_index("sub")
    y, zl, x = sub // (nz * nx), (sub // nx) % nz, sub % nx

    plane = []
    for oy in range(ny):
        for ox in range(nx):
            if oy or ox:
                qy, qx = (y + oy) % ny, (x + ox) % nx
                plane.append({"sub": qy * (nz * nx) + zl * nx + qx})
    column = []
    for oz in range(nz):
        for oa in range(N_ALT):
            if oz or oa:
                qz, qa = (zl + oz) % nz, (me + oa) % N_ALT
                column.append({"sub": y * (nz * nx) + qz * nx + x, "alt": qa})
    my_plane = y * nx + x
    my_column = zl * N_ALT + me

    barrier = pltpu.get_barrier_semaphore()
    for device in plane + column:
        pl.semaphore_signal(barrier, inc=1, device_id=device, device_id_type=MESH)

    loads = []
    for src, dst in (
        (ph_hbm, ph_in), (amp_hbm, amp_in), (cot_hbm, cot_in), (pos_hbm, pos_ref),
        (prof_hbm, prof_ref), (wt_hbm, wt_ref), (tab_hbm, tab),
    ):
        cp = pltpu.make_async_copy(src, dst, load_sem.at[len(loads)])
        cp.start()
        loads.append(cp)

    loads[0].wait()
    t = jnp.concatenate(swap4([ph_in[32 * k : 32 * k + 32, :] for k in range(4)]), axis=0).T
    ph_send[...] = t.reshape(8, 16, LANES)
    loads[1].wait()
    amp = amp_in[...].astype(F32)
    t = jnp.concatenate(swap4([amp[32 * k : 32 * k + 32, :] for k in range(4)]), axis=0).T
    amp_send[...] = t.reshape(8, 16, LANES).astype(BF16)

    loads[4].wait()
    loads[5].wait()
    row = lax.broadcasted_iota(jnp.int32, (8, LANES), 0)
    lane = lax.broadcasted_iota(jnp.int32, (8, LANES), 1)
    small = jnp.zeros((8, LANES), F32)
    for b in range(2):
        here = lane == 2 * me + b
        small = jnp.where(here & (row == 0), prof_ref[b], small)
        small = jnp.where(here & (row == 1), wt_ref[b], small)
    small_send[...] = small

    pl.semaphore_wait(barrier, len(plane) + len(column))

    order = [(2, 0), (2, 1), (1, 0), (3, 0), (1, 1), (3, 1), (0, 1)]
    kinds = ((small_send, small_recv), (ph_send, ph_recv), (amp_send, amp_recv), (cot_send, cot_recv), (back_send, back_recv))

    def peer_of(offset):
        return (me // 2 + offset[0]) % (N_ALT // 2) * 2 + (me + offset[1]) % 2

    def exchange(kind, offset):
        src, dst = kinds[kind]
        peer = peer_of(offset)
        return pltpu.make_async_remote_copy(
            src_ref=src if kind == 0 else src.at[peer],
            dst_ref=dst.at[me],
            send_sem=send_sem.at[kind],
            recv_sem=recv_sem.at[kind],
            device_id={"alt": peer},
            device_id_type=MESH,
        )

    def start(kind):
        for offset in order:
            exchange(kind, offset).start()

    def wait_in(kind):
        dst = kinds[kind][1].at[pl.ds(0, N_ALT - 1)]
        pltpu.make_async_copy(dst, dst, recv_sem.at[kind]).wait()

    def wait_out(kind):
        dst = kinds[kind][1].at[pl.ds(0, N_ALT - 1)]
        pltpu.make_async_copy(dst, dst, send_sem.at[kind]).wait()

    start(0)
    start(1)
    start(2)

    loads[2].wait()
    for half in range(2):
        z = swap4([cot_in[256 * half + 64 * k : 256 * half + 64 * k + 64, :].astype(F32) for k in range(4)])
        for u in range(2):
            t = jnp.concatenate([z[2 * u], z[2 * u + 1]], axis=0).T
            cot_send[:, 16 * half : 16 * half + 16, LANES * u : LANES * u + LANES] = t.reshape(8, 16, LANES).astype(BF16)
    start(3)

    small_recv[me] = small
    ph_recv[me] = ph_send[me]
    amp_recv[me] = amp_send[me]
    cot_recv[me] = cot_send[me]

    src = lax.broadcasted_iota(jnp.int32, (LANES, 4 * LANES), 0)
    dst = lax.broadcasted_iota(jnp.int32, (LANES, 4 * LANES), 1)
    pick = (src == 16 * me + 4 * ((dst % LANES) // 32) + dst // LANES).astype(F32)
    loads[3].wait()
    pos = jnp.concatenate([pos_ref[...], jnp.zeros((6, LANES), F32)], axis=0)
    pos = jnp.dot(pos, pick, precision=lax.Precision.HIGHEST, preferred_element_type=F32)
    r64 = lax.broadcasted_iota(jnp.int32, (N_FIELD, LANES), 0)
    l64 = lax.broadcasted_iota(jnp.int32, (N_FIELD, LANES), 1)
    dr = jnp.where(r64 < 32, r64, r64 - N_FIELD).astype(F32)
    dc = (l64 % 32).astype(F32)
    twice = jnp.where(l64 % 32 == 0, 1.0, 2.0).astype(F32)
    for g in range(4):
        px = pos[0:1, LANES * g : LANES * g + LANES]
        py = pos[1:2, LANES * g : LANES * g + LANES]
        s, c = sincos(0.05 * (px * dc + py * dr))
        c2, s2 = c * c - s * s, 2.0 * s * c
        for j in range(8):
            ct[j, g], sn[j, g] = c, s
            if j < 7:
                c, s = c * c2 - s * s2, s * c2 + c * s2

    wait_in(0)
    bins = small_recv[0]
    for k in range(1, N_ALT):
        bins = bins + small_recv[k]
    prof, wt = bins[0:1, :], bins[1:2, :]
    total = jnp.sum(prof, axis=1, keepdims=True)
    omega = prof * wt / total
    for g in range(4):
        re = jnp.zeros((N_FIELD, LANES), F32)
        im = jnp.zeros((N_FIELD, LANES), F32)
        for j in range(8):
            up, down = omega[:, 8 + j : 9 + j], omega[:, 7 - j : 8 - j]
            re = re + (up + down) * ct[j, g]
            im = im - (up - down) * sn[j, g]
        sf[0, g] = re * twice
        sf[1, g] = im * twice

    loads[6].wait()
    wait_in(1)
    wait_in(2)
    s, c = sincos(ph_recv[...].reshape(LANES, LANES))
    amp = amp_recv[...].astype(F32).reshape(LANES, LANES)
    e_re, e_im = amp * c, amp * s
    er[...] = e_re
    ei[...] = e_im
    e_both = split(jnp.concatenate([e_re, e_im], axis=1))
    for h in range(2):
        half = lane_mm(e_both, tab, W1[h])
        yu[2 * h], yu[2 * h + 1] = half[:, :LANES], half[:, LANES:]
    a2, a3 = tab[A2 : A2 + LANES, :192], tab[A3 : A3 + LANES, :192]
    power = []
    for g in range(4):
        m = [yu.at[k][pl.ds(g, 32, stride=4), :] for k in range(4)]
        m = [jnp.concatenate([m[0], m[1]], axis=1), jnp.concatenate([m[2], m[3]], axis=1)]
        u = row_mm(a2, jnp.concatenate(m, axis=0))
        uf[g] = u
        power.append(u[:64] * u[:64] + u[64:] * u[64:])
    yb = lane_mm(split(jnp.concatenate(power, axis=0)), tab, W3)
    keep = jnp.where(r64 == 32, 0.0, twice) * (1.0 / (1024.0 * 4096.0))
    for g in range(4):
        v = row_mm(a3, yb[64 * g : 64 * g + 64, :])
        bw[0, g] = (v[:64, :LANES] - v[64:, LANES:]) * keep
        bw[1, g] = (v[:64, LANES:] + v[64:, :LANES]) * keep

    wait_in(3)
    cot = cot_recv[...].reshape(256, 256)
    yy = mm(cot, tab[W3 : W3 + 256, :]) + mm(cot, tab[W3 + 256 : W3 + 512, :])
    yg[0], yg[1] = yy[:, :LANES], yy[:, LANES:]
    for g in range(4):
        m = [yg.at[k][pl.ds(g, 64, stride=4), :] for k in range(2)]
        v = row_mm(a3, jnp.concatenate(m, axis=1))
        g_re = v[:64, :LANES] - v[64:, LANES:]
        g_im = v[:64, LANES:] + v[64:, :LANES]
        b_re, b_im, s_re, s_im = bw[0, g], bw[1, g], sf[0, g], sf[1, g]
        qf[0, g] = g_re * b_re + g_im * b_im
        qf[1, g] = g_im * b_re - g_re * b_im
        gf[g] = jnp.concatenate([g_re * s_re - g_im * s_im, g_re * s_im + g_im * s_re], axis=1)

    sums = []
    for part, table in ((0, ct), (1, sn)):
        rows = []
        for j in range(8):
            acc = jnp.zeros((8, LANES), F32)
            for g in range(4):
                acc = acc + jnp.sum((qf[part, g] * table[j, g]).reshape(8, 8, LANES), axis=0)
            rows.append(jnp.sum(acc, axis=0, keepdims=True))
        sums.append(jnp.sum(jnp.concatenate(rows, axis=0), axis=1, keepdims=True))
    here = jnp.where(lane == 8 + row, sums[0] + sums[1], 0.0) + jnp.where(lane == 7 - row, sums[0] - sums[1], 0.0)
    mine = jnp.sum(here, axis=0, keepdims=True)
    row_a[...] = mine
    st_a[my_plane] = mine

    def post(peers, me_slot, src, dst, sems):
        for device in peers:
            pltpu.make_async_remote_copy(
                src_ref=src, dst_ref=dst.at[me_slot], send_sem=sems.at[0], recv_sem=sems.at[1],
                device_id=device, device_id_type=MESH,
            ).start()

    def wait_all(peers, dst, sem):
        if peers:
            part = dst.at[pl.ds(0, len(peers))]
            pltpu.make_async_copy(part, part, sem).wait()

    post(plane, my_plane, row_a, st_a, sems_a)

    z = []
    for g in range(4):
        v = row_mm(a3, gf[g])
        z.append(jnp.concatenate([v[:64, :LANES] + v[64:, LANES:], v[:64, LANES:] - v[64:, :LANES]], axis=1))
    g_hat = lane_mm(split(jnp.concatenate(z, axis=0)), tab, W4)
    for g in range(4):
        gh = g_hat[64 * g : 64 * g + 64, :]
        v = jnp.concatenate([uf[g, :64, :] * gh, uf[g, 64:, :] * gh], axis=0)
        hi, lo = split(v)
        v = mm(tab[A5 : A5 + 64, :], jnp.concatenate([hi, lo], axis=0)) + mm(tab[A5 + 64 : A5 + 128, :LANES], hi)
        for k in range(2):
            cs.at[k][pl.ds(g, 32, stride=4), :] = v[:32, LANES * k : LANES * k + LANES]
            cs.at[2 + k][pl.ds(g, 32, stride=4), :] = v[32:, LANES * k : LANES * k + LANES]
    conv = sum(lane_mm(split(jnp.concatenate([cs[2 * h], cs[2 * h + 1]], axis=1)), tab, W5[h]) for h in range(2))
    grad = (er[...] * conv[:, LANES:] - ei[...] * conv[:, :LANES]) * (2.0 / (1024.0 * 4096.0))
    back_send[...] = grad.reshape(8, 16, LANES)
    start(4)
    back_recv[me] = back_send[me]

    wait_all(plane, st_a, sems_a.at[1])
    acc = st_a[0]
    for k in range(1, ny * nx):
        acc = acc + st_a[k]
    row_b[...] = acc
    st_b[my_column] = acc
    post(column, my_column, row_b, st_b, sems_b)

    wait_in(4)
    m = back_recv[...].reshape(LANES, LANES).T
    rows = swap4([m[32 * k : 32 * k + 32, :] for k in range(4)])
    for k in range(4):
        grad_ref[32 * k : 32 * k + 32, :] = rows[k]

    wait_all(column, st_b, sems_b.at[1])
    stat = st_b[0]
    for k in range(1, nz * N_ALT):
        stat = stat + st_b[k]
    bins_ref[...] = jnp.concatenate([prof, wt, stat, total * jnp.ones((1, LANES), F32), jnp.zeros((4, LANES), F32)], axis=0)

    for kind in range(5):
        wait_out(kind)
    wait_all(plane, st_a, sems_a.at[0])
    wait_all(column, st_b, sems_b.at[0])


def finish(n_all, grad_ref, bins_ref, out_hbm, pg_ref, sem):
    copy = pltpu.make_async_copy(grad_ref, out_hbm, sem)
    copy.start()
    me = lax.axis_index("alt")
    lane = lax.broadcasted_iota(jnp.int32, (1, LANES), 1)
    prof, wt, stat, total = (bins_ref[k : k + 1, :] for k in range(4))
    centre = jnp.sum(prof * wt * stat, axis=1, keepdims=True)
    pg = (wt * stat / total - centre / (total * total)) * (1.0 / n_all)
    for b in range(2):
        pg_ref[b] = jnp.sum(jnp.where(lane == 2 * me + b, pg, 0.0))
    copy.wait()


def local(dims, cotangent, amplitude, phase, position, profile, alt_weight):
    tables = jnp.asarray(make_tables())
    any_spec = pl.BlockSpec(memory_space=pl.ANY)
    vmem = pl.BlockSpec(memory_space=pltpu.VMEM)
    smem = pl.BlockSpec(memory_space=pltpu.SMEM)
    n_plane, n_column = dims[0] * dims[2], dims[1] * N_ALT
    dma = pltpu.SemaphoreType.DMA
    back, bins = pl.pallas_call(
        functools.partial(kernel, dims),
        out_shape=(pltpu.VMEM((LANES, LANES), F32), pltpu.VMEM((8, LANES), F32)),
        in_specs=[any_spec] * 7,
        out_specs=(vmem, vmem),
        scratch_shapes=[
            pltpu.VMEM((512, LANES), BF16), pltpu.VMEM((LANES, LANES), BF16), pltpu.VMEM((LANES, LANES), F32), pltpu.VMEM((2, LANES), F32),
            pltpu.VMEM(tables.shape, BF16), pltpu.SMEM((2,), F32), pltpu.SMEM((2,), F32),
            pltpu.VMEM((8, 32, 256), BF16), pltpu.VMEM((8, 16, LANES), BF16), pltpu.VMEM((8, 16, LANES), F32), pltpu.VMEM((8, LANES), F32),
            pltpu.VMEM((8, 32, 256), BF16), pltpu.VMEM((8, 16, LANES), BF16), pltpu.VMEM((8, 16, LANES), F32), pltpu.VMEM((8, 8, LANES), F32),
            pltpu.VMEM((8, 16, LANES), F32), pltpu.VMEM((8, 16, LANES), F32),
            pltpu.VMEM((n_plane, 1, LANES), F32), pltpu.VMEM((n_column, 1, LANES), F32),
            pltpu.VMEM((1, LANES), F32), pltpu.VMEM((1, LANES), F32),
            pltpu.VMEM((4, LANES, LANES), F32), pltpu.VMEM((4, LANES, 256), F32), pltpu.VMEM((2, 4, 64, LANES), F32),
            pltpu.VMEM((2, 256, LANES), F32), pltpu.VMEM((4, LANES, LANES), F32), pltpu.VMEM((4, 64, 256), F32),
            pltpu.VMEM((2, 4, 64, LANES), F32),
            pltpu.VMEM((8, 4, 64, LANES), F32), pltpu.VMEM((8, 4, 64, LANES), F32),
            pltpu.VMEM((LANES, LANES), F32), pltpu.VMEM((LANES, LANES), F32),
            pltpu.VMEM((2, 4, 64, LANES), F32),
            dma((7,)), dma((5,)), dma((5,)), dma((2,)), dma((2,)),
        ],
        compiler_params=pltpu.CompilerParams(collective_id=0, has_side_effects=True),
    )(cotangent, amplitude, phase, position, profile, alt_weight, tables)
    return pl.pallas_call(
        functools.partial(finish, dims[0] * dims[1] * dims[2] * LANES),
        out_shape=(jax.ShapeDtypeStruct((LANES, LANES), F32), jax.ShapeDtypeStruct((2,), F32)),
        in_specs=[vmem, vmem],
        out_specs=(any_spec, smem),
        scratch_shapes=[pltpu.SemaphoreType.DMA],
    )(*(pltpu.with_memory_space_constraint(v, pltpu.VMEM) for v in (back, bins)))


def solution(mesh):
    dims = {32: (4, 2, 4), 2: (2, 1, 1)}[mesh.shape["sub"]]
    placed = (P("alt", "sub"), P("alt", "sub"), P("alt", "sub"), P(None, "sub"), P("alt"), P("alt"))
    return jax.shard_map(
        functools.partial(local, dims), mesh=mesh, in_specs=placed, out_specs=(P("alt", "sub"), P("alt")), check_vma=False
    )
```

time: 35.5 us -> 31.4 us (0.88)
  Pallas kernels: 32.7 us -> 30.7 us
  local copies, waits for them, and re-layouts: 1.99 us -> 0 us
    unnamed x4 -> x0, local copies, waits for them, and re-layouts: 1.99 us -> none
    pallas_call x1 -> x2, Pallas kernels: 32.7 us -> 30.7 us  [the longest x1 29.5 us: local(): pl.pallas_call(functools.partial(kernel, dims), out_shape=(pltpu.VMEM((LA...]
where the time goes in v2:
time: 31.4 us; the launch traced here: 31.3 us
  Pallas kernels  30.7 us (98%)
  between operations  0.64 us (2%)
    pallas_call x1, Pallas kernels, local(): pl.pallas_call(functools.partial(kernel, dims), out_shape=(pltpu.VMEM((LA...  29.5 us
    pallas_call x1, Pallas kernels, local(): pl.pallas_call(functools.partial(finish, dims[0] * dims[1] * dims[2] * LA...  1.16 us

profile of v2, /device:TPU:1, one launch (start us, length us, event | category | flops | bytes accessed | tf_op | source)
XLA Modules:
  0.0 31.3 jit_solution(913288173378378363)
XLA Ops:
  0.6 29.5 %shard_map.86 = (f32[128,128]{1,0:T(8,128)S(1)}, f32[8,128]{1,0:T(8,128)S(1)}) custom-call(bf16[512,128]{1,0:T(8,128)(2,1)} %cot_hbm.1, bf16[128,128]{1,0:T(8,128)(2,1)} %amp_hbm.1, f32[128,128]{1,0:T(8,128)} %ph_hbm.1, f32[2,128]{1,0:T(2,128)} %pos_hbm.1, f32[2]{0:T(128)} %prof_hbm.1, f32[2]{0:T(128)} %wt_hbm.1, bf16[3456,256]{1,0:T(8,128)(2,1)} %constant.2.clone.tab_hbm), custom_call_target="tpu_custom_call" | custom-call | tf_op jit(solution)/shard_map/pallas_call | solution.py:399
  30.2 1.2 %shard_map.87 = (f32[128,128]{1,0:T(8,128)}, f32[2]{0:T(128)}) custom-call(f32[128,128]{1,0:T(8,128)S(1)} %get-tuple-element.4.grad_ref, f32[8,128]{1,0:T(8,128)S(1)} %get-tuple-element.5.bins_ref), custom_call_target="tpu_custom_call" | custom-call | tf_op jit(solution)/shard_map/pallas_call | solution.py:422

commit v3 on v2

--- a/solution.py
+++ b/solution.py
@@ -110,6 +110,10 @@
     return z0, z1, z2, z3
 
 
+def far_first(n):
+    return sorted(range(n), key=lambda o: -min(o, n - o))
+
+
 def kernel(
     dims,
     cot_hbm, amp_hbm, ph_hbm, pos_hbm, prof_hbm, wt_hbm,
@@ -129,32 +133,36 @@
     y, zl, x = sub // (nz * nx), (sub // nx) % nz, sub % nx
 
     plane = []
-    for oy in range(ny):
-        for ox in range(nx):
+    for oy in far_first(ny):
+        for ox in far_first(nx):
             if oy or ox:
                 qy, qx = (y + oy) % ny, (x + ox) % nx
                 plane.append({"sub": qy * (nz * nx) + zl * nx + qx})
     column = []
-    for oz in range(nz):
-        for oa in range(N_ALT):
-            if oz or oa:
-                qz, qa = (zl + oz) % nz, (me + oa) % N_ALT
-                column.append({"sub": y * (nz * nx) + qz * nx + x, "alt": qa})
+    for oh in far_first(N_ALT // 2):
+        for oz in range(nz):
+            for oc in range(2):
+                if oh or oz or oc:
+                    qz, qa = (zl + oz) % nz, (me // 2 + oh) % (N_ALT // 2) * 2 + (me + oc) % 2
+                    column.append({"sub": y * (nz * nx) + qz * nx + x, "alt": qa})
     my_plane = y * nx + x
     my_column = zl * N_ALT + me
-
-    barrier = pltpu.get_barrier_semaphore()
-    for device in plane + column:
-        pl.semaphore_signal(barrier, inc=1, device_id=device, device_id_type=MESH)
 
     loads = []
     for src, dst in (
         (ph_hbm, ph_in), (amp_hbm, amp_in), (cot_hbm, cot_in), (pos_hbm, pos_ref),
         (prof_hbm, prof_ref), (wt_hbm, wt_ref), (tab_hbm, tab),
     ):
-        cp = pltpu.make_async_copy(src, dst, load_sem.at[len(loads)])
+        loads.append(pltpu.make_async_copy(src, dst, load_sem.at[len(loads)]))
+    loads[0].start()
+    loads[1].start()
+
+    barrier = pltpu.get_barrier_semaphore()
+    for device in column + plane:
+        pl.semaphore_signal(barrier, inc=1, device_id=device, device_id_type=MESH)
+
+    for cp in loads[2:]:
         cp.start()
-        loads.append(cp)
 
     loads[0].wait()
     t = jnp.concatenate(swap4([ph_in[32 * k : 32 * k + 32, :] for k in range(4)]), axis=0).T
@@ -168,11 +176,10 @@
     loads[5].wait()
     row = lax.broadcasted_iota(jnp.int32, (8, LANES), 0)
     lane = lax.broadcasted_iota(jnp.int32, (8, LANES), 1)
-    small = jnp.zeros((8, LANES), F32)
+    small = jnp.zeros((1, LANES), F32)
     for b in range(2):
-        here = lane == 2 * me + b
-        small = jnp.where(here & (row == 0), prof_ref[b], small)
-        small = jnp.where(here & (row == 1), wt_ref[b], small)
+        small = jnp.where(lane[:1] == 2 * me + b, prof_ref[b], small)
+        small = jnp.where(lane[:1] == N_BINS + 2 * me + b, wt_ref[b], small)
     small_send[...] = small
 
     pl.semaphore_wait(barrier, len(plane) + len(column))
@@ -249,7 +256,8 @@
     bins = small_recv[0]
     for k in range(1, N_ALT):
         bins = bins + small_recv[k]
-    prof, wt = bins[0:1, :], bins[1:2, :]
+    prof = jnp.where(lane[:1] < N_BINS, bins, 0.0)
+    wt = jnp.where(lane[:1] < N_BINS, pltpu.roll(bins, LANES - N_BINS, 1), 0.0)
     total = jnp.sum(prof, axis=1, keepdims=True)
     omega = prof * wt / total
     for g in range(4):
@@ -298,10 +306,10 @@
         v = row_mm(a3, jnp.concatenate(m, axis=1))
         g_re = v[:64, :LANES] - v[64:, LANES:]
         g_im = v[:64, LANES:] + v[64:, :LANES]
-        b_re, b_im, s_re, s_im = bw[0, g], bw[1, g], sf[0, g], sf[1, g]
+        b_re, b_im = bw[0, g], bw[1, g]
         qf[0, g] = g_re * b_re + g_im * b_im
         qf[1, g] = g_im * b_re - g_re * b_im
-        gf[g] = jnp.concatenate([g_re * s_re - g_im * s_im, g_re * s_im + g_im * s_re], axis=1)
+        gf[g] = jnp.concatenate([g_re, g_im], axis=1)
 
     sums = []
     for part, table in ((0, ct), (1, sn)):
@@ -315,7 +323,7 @@
     here = jnp.where(lane == 8 + row, sums[0] + sums[1], 0.0) + jnp.where(lane == 7 - row, sums[0] - sums[1], 0.0)
     mine = jnp.sum(here, axis=0, keepdims=True)
     row_a[...] = mine
-    st_a[my_plane] = mine
+    st_a[my_column] = mine
 
     def post(peers, me_slot, src, dst, sems):
         for device in peers:
@@ -329,11 +337,12 @@
             part = dst.at[pl.ds(0, len(peers))]
             pltpu.make_async_copy(part, part, sem).wait()
 
-    post(plane, my_plane, row_a, st_a, sems_a)
+    post(column, my_column, row_a, st_a, sems_a)
 
     z = []
     for g in range(4):
-        v = row_mm(a3, gf[g])
+        g_re, g_im, s_re, s_im = gf[g, :, :LANES], gf[g, :, LANES:], sf[0, g], sf[1, g]
+        v = row_mm(a3, jnp.concatenate([g_re * s_re - g_im * s_im, g_re * s_im + g_im * s_re], axis=1))
         z.append(jnp.concatenate([v[:64, :LANES] + v[64:, LANES:], v[:64, LANES:] - v[64:, :LANES]], axis=1))
     g_hat = lane_mm(split(jnp.concatenate(z, axis=0)), tab, W4)
     for g in range(4):
@@ -350,13 +359,13 @@
     start(4)
     back_recv[me] = back_send[me]
 
-    wait_all(plane, st_a, sems_a.at[1])
+    wait_all(column, st_a, sems_a.at[1])
     acc = st_a[0]
-    for k in range(1, ny * nx):
+    for k in range(1, nz * N_ALT):
         acc = acc + st_a[k]
     row_b[...] = acc
-    st_b[my_column] = acc
-    post(column, my_column, row_b, st_b, sems_b)
+    st_b[my_plane] = acc
+    post(plane, my_plane, row_b, st_b, sems_b)
 
     wait_in(4)
     m = back_recv[...].reshape(LANES, LANES).T
@@ -364,50 +373,49 @@
     for k in range(4):
         grad_ref[32 * k : 32 * k + 32, :] = rows[k]
 
-    wait_all(column, st_b, sems_b.at[1])
+    wait_all(plane, st_b, sems_b.at[1])
     stat = st_b[0]
-    for k in range(1, nz * N_ALT):
+    for k in range(1, ny * nx):
         stat = stat + st_b[k]
-    bins_ref[...] = jnp.concatenate([prof, wt, stat, total * jnp.ones((1, LANES), F32), jnp.zeros((4, LANES), F32)], axis=0)
+    centre = jnp.sum(prof * wt * stat, axis=1, keepdims=True)
+    pg = (wt * stat / total - centre / (total * total)) * (1.0 / (ny * nz * nx * LANES))
+    own = [jnp.sum(jnp.where(lane[:1] == 2 * me + b, pg, 0.0), axis=1, keepdims=True) for b in range(2)]
+    bins_ref[...] = jnp.where(lane[:1] == 0, own[0], own[1])
 
     for kind in range(5):
         wait_out(kind)
-    wait_all(plane, st_a, sems_a.at[0])
-    wait_all(column, st_b, sems_b.at[0])
-
-
-def finish(n_all, grad_ref, bins_ref, out_hbm, pg_ref, sem):
-    copy = pltpu.make_async_copy(grad_ref, out_hbm, sem)
-    copy.start()
-    me = lax.axis_index("alt")
-    lane = lax.broadcasted_iota(jnp.int32, (1, LANES), 1)
-    prof, wt, stat, total = (bins_ref[k : k + 1, :] for k in range(4))
-    centre = jnp.sum(prof * wt * stat, axis=1, keepdims=True)
-    pg = (wt * stat / total - centre / (total * total)) * (1.0 / n_all)
-    for b in range(2):
-        pg_ref[b] = jnp.sum(jnp.where(lane == 2 * me + b, pg, 0.0))
-    copy.wait()
+    wait_all(column, st_a, sems_a.at[0])
+    wait_all(plane, st_b, sems_b.at[0])
+
+
+def finish(grad_ref, bins_ref, out_hbm, pg_hbm, pg_ref, sems):
+    copies = [pltpu.make_async_copy(grad_ref, out_hbm, sems.at[0]), pltpu.make_async_copy(pg_ref, pg_hbm, sems.at[1])]
+    copies[0].start()
+    pg_ref[0] = bins_ref[0, 0]
+    pg_ref[1] = bins_ref[0, 1]
+    copies[1].start()
+    for cp in copies:
+        cp.wait()
 
 
 def local(dims, cotangent, amplitude, phase, position, profile, alt_weight):
     tables = jnp.asarray(make_tables())
     any_spec = pl.BlockSpec(memory_space=pl.ANY)
     vmem = pl.BlockSpec(memory_space=pltpu.VMEM)
-    smem = pl.BlockSpec(memory_space=pltpu.SMEM)
     n_plane, n_column = dims[0] * dims[2], dims[1] * N_ALT
     dma = pltpu.SemaphoreType.DMA
     back, bins = pl.pallas_call(
         functools.partial(kernel, dims),
-        out_shape=(pltpu.VMEM((LANES, LANES), F32), pltpu.VMEM((8, LANES), F32)),
+        out_shape=(pltpu.VMEM((LANES, LANES), F32), pltpu.VMEM((1, LANES), F32)),
         in_specs=[any_spec] * 7,
         out_specs=(vmem, vmem),
         scratch_shapes=[
             pltpu.VMEM((512, LANES), BF16), pltpu.VMEM((LANES, LANES), BF16), pltpu.VMEM((LANES, LANES), F32), pltpu.VMEM((2, LANES), F32),
             pltpu.VMEM(tables.shape, BF16), pltpu.SMEM((2,), F32), pltpu.SMEM((2,), F32),
-            pltpu.VMEM((8, 32, 256), BF16), pltpu.VMEM((8, 16, LANES), BF16), pltpu.VMEM((8, 16, LANES), F32), pltpu.VMEM((8, LANES), F32),
-            pltpu.VMEM((8, 32, 256), BF16), pltpu.VMEM((8, 16, LANES), BF16), pltpu.VMEM((8, 16, LANES), F32), pltpu.VMEM((8, 8, LANES), F32),
+            pltpu.VMEM((8, 32, 256), BF16), pltpu.VMEM((8, 16, LANES), BF16), pltpu.VMEM((8, 16, LANES), F32), pltpu.VMEM((1, LANES), F32),
+            pltpu.VMEM((8, 32, 256), BF16), pltpu.VMEM((8, 16, LANES), BF16), pltpu.VMEM((8, 16, LANES), F32), pltpu.VMEM((8, 1, LANES), F32),
             pltpu.VMEM((8, 16, LANES), F32), pltpu.VMEM((8, 16, LANES), F32),
-            pltpu.VMEM((n_plane, 1, LANES), F32), pltpu.VMEM((n_column, 1, LANES), F32),
+            pltpu.VMEM((n_column, 1, LANES), F32), pltpu.VMEM((n_plane, 1, LANES), F32),
             pltpu.VMEM((1, LANES), F32), pltpu.VMEM((1, LANES), F32),
             pltpu.VMEM((4, LANES, LANES), F32), pltpu.VMEM((4, LANES, 256), F32), pltpu.VMEM((2, 4, 64, LANES), F32),
             pltpu.VMEM((2, 256, LANES), F32), pltpu.VMEM((4, LANES, LANES), F32), pltpu.VMEM((4, 64, 256), F32),
@@ -420,11 +428,11 @@
         compiler_params=pltpu.CompilerParams(collective_id=0, has_side_effects=True),
     )(cotangent, amplitude, phase, position, profile, alt_weight, tables)
     return pl.pallas_call(
-        functools.partial(finish, dims[0] * dims[1] * dims[2] * LANES),
+        finish,
         out_shape=(jax.ShapeDtypeStruct((LANES, LANES), F32), jax.ShapeDtypeStruct((2,), F32)),
         in_specs=[vmem, vmem],
-        out_specs=(any_spec, smem),
-        scratch_shapes=[pltpu.SemaphoreType.DMA],
+        out_specs=(any_spec, any_spec),
+        scratch_shapes=[pltpu.SMEM((2,), F32), dma((2,))],
     )(*(pltpu.with_memory_space_constraint(v, pltpu.VMEM) for v in (back, bins)))
 
 

time: 31.4 us -> 29.5 us (0.939)
  Pallas kernels: 30.7 us -> 28.8 us
    pallas_call x1, Pallas kernels: 29.5 us -> 28.1 us  [local(): pl.pallas_call(functools.partial(kernel, dims), out_shape=(pltpu.VMEM((LA...]
    pallas_call x1, Pallas kernels: 1.16 us -> 0.66 us  [local(): pl.pallas_call(finish, out_shape=(jax.ShapeDtypeStruct((LANES, LANES), F3...]
where the time goes in v3:
time: 29.5 us; the launch traced here: 29.4 us
  Pallas kernels  28.8 us (98%)
  between operations  0.64 us (2%)
    pallas_call x1, Pallas kernels, local(): pl.pallas_call(functools.partial(kernel, dims), out_shape=(pltpu.VMEM((LA...  28.1 us
    pallas_call x1, Pallas kernels, local(): pl.pallas_call(finish, out_shape=(jax.ShapeDtypeStruct((LANES, LANES), F3...  0.66 us

profile of v3, /device:TPU:1, one launch (start us, length us, event | category | flops | bytes accessed | tf_op | source)
XLA Modules:
  0.0 29.4 jit_solution(1927287790214366836)
XLA Ops:
  0.6 28.1 %shard_map.86 = (f32[128,128]{1,0:T(8,128)S(1)}, f32[1,128]{1,0:T(1,128)S(1)}) custom-call(bf16[512,128]{1,0:T(8,128)(2,1)} %cot_hbm.1, bf16[128,128]{1,0:T(8,128)(2,1)} %amp_hbm.1, f32[128,128]{1,0:T(8,128)} %ph_hbm.1, f32[2,128]{1,0:T(2,128)} %pos_hbm.1, f32[2]{0:T(128)} %prof_hbm.1, f32[2]{0:T(128)} %wt_hbm.1, bf16[3456,256]{1,0:T(8,128)(2,1)} %constant.2.clone.tab_hbm), custom_call_target="tpu_custom_call" | custom-call | tf_op jit(solution)/shard_map/pallas_call | solution.py:407
  28.7 0.7 %shard_map.87 = (f32[128,128]{1,0:T(8,128)}, f32[2]{0:T(128)}) custom-call(f32[128,128]{1,0:T(8,128)S(1)} %get-tuple-element.4.grad_ref, f32[1,128]{1,0:T(1,128)S(1)} %get-tuple-element.5.bins_ref), custom_call_target="tpu_custom_call" | custom-call | tf_op jit(solution)/shard_map/pallas_call | solution.py:430

commit v4 on v3

--- a/solution.py
+++ b/solution.py
@@ -37,12 +37,13 @@
     w4 = w3.T
     w5 = np.block([[kc, ks], [-ks, kc]])
     a2 = np.block([[half_c, half_s], [-half_s, half_c]])
-    a3 = np.vstack([cos, sin])
+    a3 = np.vstack([half_c.T, half_s.T])
+    a4 = np.block([[half_c, 0 * half_c], [0 * half_s, half_s]])
     a5 = np.block([[cos[:N_PUPIL], -sin[:N_PUPIL]], [sin[:N_PUPIL], cos[:N_PUPIL]]])
     blocks = []
     for w in (w1[:, :256], w1[:, 256:], w3, w4, w5[:256], w5[256:]):
         blocks += list(split_np(w))
-    for a in (a2, a3):
+    for a in (a2, a4, a3):
         hi, lo = split_np(a)
         blocks.append(np.concatenate([hi, hi, lo, np.zeros_like(lo)], axis=1))
     hi, lo = split_np(a5)
@@ -51,7 +52,7 @@
 
 
 W1, W3, W4, W5 = (0, 512), 1024, 1536, (2048, 2560)
-A2, A3, A5 = 3072, 3200, 3328
+A2, A4, A3, A5 = 3072, 3200, 3328, 3392
 
 
 def split(x):
@@ -73,6 +74,11 @@
 def row_mm(table, x):
     hi, lo = split(x)
     return mm(table, jnp.concatenate([hi, lo, hi], axis=0))
+
+
+def both_signs(v):
+    c_re, c_im, s_re, s_im = v[:32, :LANES], v[:32, LANES:], v[32:, :LANES], v[32:, LANES:]
+    return jnp.concatenate([c_re - s_im, c_re + s_im], axis=0), jnp.concatenate([c_im + s_re, c_im - s_re], axis=0)
 
 
 def sincos(x):
@@ -124,27 +130,30 @@
     cot_send, amp_send, ph_send, small_send,
     cot_recv, amp_recv, ph_recv, small_recv,
     back_send, back_recv, st_a, st_b, row_a, row_b,
-    yu, uf, bw, yg, cs, gf, qf, ct, sn, er, ei, sf,
+    yu, uf, bw, yg, cs, gf, yt, xt, ct, sn, er, ei, sf,
     load_sem, send_sem, recv_sem, sems_a, sems_b,
 ):
     ny, nz, nx = dims
     me = lax.axis_index("alt")
     sub = lax.axis_index("sub")
-    y, zl, x = sub // (nz * nx), (sub // nx) % nz, sub % nx
-
-    plane = []
-    for oy in far_first(ny):
-        for ox in far_first(nx):
-            if oy or ox:
-                qy, qx = (y + oy) % ny, (x + ox) % nx
-                plane.append({"sub": qy * (nz * nx) + zl * nx + qx})
-    column = []
-    for oh in far_first(N_ALT // 2):
-        for oz in range(nz):
-            for oc in range(2):
-                if oh or oz or oc:
-                    qz, qa = (zl + oz) % nz, (me // 2 + oh) % (N_ALT // 2) * 2 + (me + oc) % 2
-                    column.append({"sub": y * (nz * nx) + qz * nx + x, "alt": qa})
+    x, yz = lax.rem(sub, nx), lax.div(sub, nx)
+    y, zl = lax.div(yz, nz), lax.rem(yz, nz)
+    core, high = lax.rem(me, 2), lax.div(me, 2)
+    nh = N_ALT // 2
+    at_high = [2 * lax.rem(high + o, nh) for o in range(nh)]
+    at_core = [core, 1 - core]
+
+    at_y = [lax.rem(y + o, ny) * (nz * nx) + zl * nx for o in range(ny)]
+    at_x = [lax.rem(x + o, nx) for o in range(nx)]
+    plane = [{"sub": at_y[oy] + at_x[ox]} for oy in far_first(ny) for ox in far_first(nx) if oy or ox]
+    at_z = [y * (nz * nx) + lax.rem(zl + o, nz) * nx + x for o in range(nz)]
+    column = [
+        {"sub": at_z[oz], "alt": at_high[oh] + at_core[oc]}
+        for oh in far_first(nh)
+        for oz in range(nz)
+        for oc in range(2)
+        if oh or oz or oc
+    ]
     my_plane = y * nx + x
     my_column = zl * N_ALT + me
 
@@ -154,7 +163,9 @@
         (prof_hbm, prof_ref), (wt_hbm, wt_ref), (tab_hbm, tab),
     ):
         loads.append(pltpu.make_async_copy(src, dst, load_sem.at[len(loads)]))
-    loads[0].start()
+    for k in range(4):
+        part = pl.ds(32 * k, 32)
+        pltpu.make_async_copy(ph_hbm.at[part], ph_in.at[part], load_sem.at[0]).start()
     loads[1].start()
 
     barrier = pltpu.get_barrier_semaphore()
@@ -172,6 +183,12 @@
     t = jnp.concatenate(swap4([amp[32 * k : 32 * k + 32, :] for k in range(4)]), axis=0).T
     amp_send[...] = t.reshape(8, 16, LANES).astype(BF16)
 
+    loads[2].wait()
+    for half in range(2):
+        z = swap4([cot_in[256 * half + 64 * k : 256 * half + 64 * k + 64, :].astype(F32) for k in range(4)])
+        for u in range(2):
+            t = jnp.concatenate([z[2 * u], z[2 * u + 1]], axis=0).T
+            cot_send[:, 16 * half : 16 * half + 16, LANES * u : LANES * u + LANES] = t.reshape(8, 16, LANES).astype(BF16)
     loads[4].wait()
     loads[5].wait()
     row = lax.broadcasted_iota(jnp.int32, (8, LANES), 0)
@@ -188,7 +205,7 @@
     kinds = ((small_send, small_recv), (ph_send, ph_recv), (amp_send, amp_recv), (cot_send, cot_recv), (back_send, back_recv))
 
     def peer_of(offset):
-        return (me // 2 + offset[0]) % (N_ALT // 2) * 2 + (me + offset[1]) % 2
+        return at_high[offset[0]] + at_core[offset[1]]
 
     def exchange(kind, offset):
         src, dst = kinds[kind]
@@ -217,13 +234,6 @@
     start(0)
     start(1)
     start(2)
-
-    loads[2].wait()
-    for half in range(2):
-        z = swap4([cot_in[256 * half + 64 * k : 256 * half + 64 * k + 64, :].astype(F32) for k in range(4)])
-        for u in range(2):
-            t = jnp.concatenate([z[2 * u], z[2 * u + 1]], axis=0).T
-            cot_send[:, 16 * half : 16 * half + 16, LANES * u : LANES * u + LANES] = t.reshape(8, 16, LANES).astype(BF16)
     start(3)
 
     small_recv[me] = small
@@ -239,9 +249,9 @@
     pos = jnp.dot(pos, pick, precision=lax.Precision.HIGHEST, preferred_element_type=F32)
     r64 = lax.broadcasted_iota(jnp.int32, (N_FIELD, LANES), 0)
     l64 = lax.broadcasted_iota(jnp.int32, (N_FIELD, LANES), 1)
-    dr = jnp.where(r64 < 32, r64, r64 - N_FIELD).astype(F32)
+    dr = jnp.where(r64 < 32, r64, 32 - r64).astype(F32)
     dc = (l64 % 32).astype(F32)
-    twice = jnp.where(l64 % 32 == 0, 1.0, 2.0).astype(F32)
+    twice = jnp.where(r64 == 32, 0.0, jnp.where(l64 % 32 == 0, 1.0, 2.0)).astype(F32)
     for g in range(4):
         px = pos[0:1, LANES * g : LANES * g + LANES]
         py = pos[1:2, LANES * g : LANES * g + LANES]
@@ -252,6 +262,21 @@
             if j < 7:
                 c, s = c * c2 - s * s2, s * c2 + c * s2
 
+    r32 = lax.broadcasted_iota(jnp.int32, (32, LANES), 0)
+    l32 = lax.broadcasted_iota(jnp.int32, (32, LANES), 1)
+    step = 0.05 * (2 * (r32 % 8) + 1).astype(F32)
+    at = l32 % 64
+    dr_lane = jnp.where(at < 32, at, 32 - at).astype(F32)
+    for g in range(4):
+        here = l32 == 16 * me + 4 * (r32 // 8) + g
+        y_row = jnp.sum(jnp.where(here, pos_ref[1:2, :], 0.0), axis=1, keepdims=True)
+        s, c = sincos(step * y_row * dr_lane)
+        hi, lo = split(jnp.concatenate([c, s], axis=0))
+        yt[g, :, :LANES], yt[g, :, LANES:] = hi, lo
+        s, c = sincos(step * pos[0:1, LANES * g : LANES * g + LANES] * (l32 % 32).astype(F32))
+        own = r32 // 8 == l32 // 32
+        xt[g, 0], xt[g, 1] = jnp.where(own, c, 0.0), jnp.where(own, s, 0.0)
+
     wait_in(0)
     bins = small_recv[0]
     for k in range(1, N_ALT):
@@ -272,8 +297,10 @@
 
     loads[6].wait()
     wait_in(1)
+    s, c = sincos(ph_recv[...].reshape(LANES, LANES))
+    er[...], ei[...] = c, s
     wait_in(2)
-    s, c = sincos(ph_recv[...].reshape(LANES, LANES))
+    c, s = er[...], ei[...]
     amp = amp_recv[...].astype(F32).reshape(LANES, LANES)
     e_re, e_im = amp * c, amp * s
     er[...] = e_re
@@ -282,7 +309,7 @@
     for h in range(2):
         half = lane_mm(e_both, tab, W1[h])
         yu[2 * h], yu[2 * h + 1] = half[:, :LANES], half[:, LANES:]
-    a2, a3 = tab[A2 : A2 + LANES, :192], tab[A3 : A3 + LANES, :192]
+    a2, a3 = tab[A2 : A2 + LANES, :192], tab[A3 : A3 + 64, :192]
     power = []
     for g in range(4):
         m = [yu.at[k][pl.ds(g, 32, stride=4), :] for k in range(4)]
@@ -291,35 +318,35 @@
         uf[g] = u
         power.append(u[:64] * u[:64] + u[64:] * u[64:])
     yb = lane_mm(split(jnp.concatenate(power, axis=0)), tab, W3)
-    keep = jnp.where(r64 == 32, 0.0, twice) * (1.0 / (1024.0 * 4096.0))
+    keep = twice * (1.0 / (1024.0 * 4096.0))
     for g in range(4):
         v = row_mm(a3, yb[64 * g : 64 * g + 64, :])
-        bw[0, g] = (v[:64, :LANES] - v[64:, LANES:]) * keep
-        bw[1, g] = (v[:64, LANES:] + v[64:, :LANES]) * keep
+        b_re, b_im = both_signs(v)
+        bw[0, g], bw[1, g] = b_re * keep, b_im * keep
 
     wait_in(3)
     cot = cot_recv[...].reshape(256, 256)
+    parts = []
     yy = mm(cot, tab[W3 : W3 + 256, :]) + mm(cot, tab[W3 + 256 : W3 + 512, :])
     yg[0], yg[1] = yy[:, :LANES], yy[:, LANES:]
     for g in range(4):
         m = [yg.at[k][pl.ds(g, 64, stride=4), :] for k in range(2)]
         v = row_mm(a3, jnp.concatenate(m, axis=1))
-        g_re = v[:64, :LANES] - v[64:, LANES:]
-        g_im = v[:64, LANES:] + v[64:, :LANES]
+        g_re, g_im = both_signs(v)
         b_re, b_im = bw[0, g], bw[1, g]
-        qf[0, g] = g_re * b_re + g_im * b_im
-        qf[1, g] = g_im * b_re - g_re * b_im
+        hi, lo = split(jnp.concatenate([g_re * b_re + g_im * b_im, g_im * b_re - g_re * b_im], axis=1))
+        m = mm(yt[g], jnp.concatenate([hi, lo, hi, lo], axis=0))
+        parts.append((
+            xt[g, 0] * m[:32, :LANES] - xt[g, 1] * m[32:, :LANES],
+            xt[g, 1] * m[:32, LANES:] + xt[g, 0] * m[32:, LANES:],
+        ))
         gf[g] = jnp.concatenate([g_re, g_im], axis=1)
 
     sums = []
-    for part, table in ((0, ct), (1, sn)):
-        rows = []
-        for j in range(8):
-            acc = jnp.zeros((8, LANES), F32)
-            for g in range(4):
-                acc = acc + jnp.sum((qf[part, g] * table[j, g]).reshape(8, 8, LANES), axis=0)
-            rows.append(jnp.sum(acc, axis=0, keepdims=True))
-        sums.append(jnp.sum(jnp.concatenate(rows, axis=0), axis=1, keepdims=True))
+    for k in range(2):
+        acc = parts[0][k] + parts[1][k] + parts[2][k] + parts[3][k]
+        acc = acc[:8] + acc[8:16] + acc[16:24] + acc[24:]
+        sums.append(jnp.sum(acc, axis=1, keepdims=True))
     here = jnp.where(lane == 8 + row, sums[0] + sums[1], 0.0) + jnp.where(lane == 7 - row, sums[0] - sums[1], 0.0)
     mine = jnp.sum(here, axis=0, keepdims=True)
     row_a[...] = mine
@@ -339,23 +366,26 @@
 
     post(column, my_column, row_a, st_a, sems_a)
 
-    z = []
-    for g in range(4):
-        g_re, g_im, s_re, s_im = gf[g, :, :LANES], gf[g, :, LANES:], sf[0, g], sf[1, g]
-        v = row_mm(a3, jnp.concatenate([g_re * s_re - g_im * s_im, g_re * s_im + g_im * s_re], axis=1))
-        z.append(jnp.concatenate([v[:64, :LANES] + v[64:, LANES:], v[:64, LANES:] - v[64:, :LANES]], axis=1))
-    g_hat = lane_mm(split(jnp.concatenate(z, axis=0)), tab, W4)
-    for g in range(4):
-        gh = g_hat[64 * g : 64 * g + 64, :]
-        v = jnp.concatenate([uf[g, :64, :] * gh, uf[g, 64:, :] * gh], axis=0)
-        hi, lo = split(v)
-        v = mm(tab[A5 : A5 + 64, :], jnp.concatenate([hi, lo], axis=0)) + mm(tab[A5 + 64 : A5 + 128, :LANES], hi)
-        for k in range(2):
-            cs.at[k][pl.ds(g, 32, stride=4), :] = v[:32, LANES * k : LANES * k + LANES]
-            cs.at[2 + k][pl.ds(g, 32, stride=4), :] = v[32:, LANES * k : LANES * k + LANES]
-    conv = sum(lane_mm(split(jnp.concatenate([cs[2 * h], cs[2 * h + 1]], axis=1)), tab, W5[h]) for h in range(2))
-    grad = (er[...] * conv[:, LANES:] - ei[...] * conv[:, :LANES]) * (2.0 / (1024.0 * 4096.0))
-    back_send[...] = grad.reshape(8, 16, LANES)
+    @pl.when(me >= 0)
+    def _():
+        z = []
+        for g in range(4):
+            g_re, g_im, s_re, s_im = gf[g, :, :LANES], gf[g, :, LANES:], sf[0, g], sf[1, g]
+            v = jnp.concatenate([g_re * s_re - g_im * s_im, g_re * s_im + g_im * s_re], axis=1)
+            v = row_mm(tab[A4 : A4 + LANES, :192], jnp.concatenate([v[:32] + v[32:], v[:32] - v[32:]], axis=0))
+            z.append(jnp.concatenate([v[:64, :LANES] + v[64:, LANES:], v[:64, LANES:] - v[64:, :LANES]], axis=1))
+        g_hat = lane_mm(split(jnp.concatenate(z, axis=0)), tab, W4)
+        for g in range(4):
+            gh = g_hat[64 * g : 64 * g + 64, :]
+            v = jnp.concatenate([uf[g, :64, :] * gh, uf[g, 64:, :] * gh], axis=0)
+            hi, lo = split(v)
+            v = mm(tab[A5 : A5 + 64, :], jnp.concatenate([hi, lo], axis=0)) + mm(tab[A5 + 64 : A5 + 128, :LANES], hi)
+            for k in range(2):
+                cs.at[k][pl.ds(g, 32, stride=4), :] = v[:32, LANES * k : LANES * k + LANES]
+                cs.at[2 + k][pl.ds(g, 32, stride=4), :] = v[32:, LANES * k : LANES * k + LANES]
+        conv = sum(lane_mm(split(jnp.concatenate([cs[2 * h], cs[2 * h + 1]], axis=1)), tab, W5[h]) for h in range(2))
+        grad = (er[...] * conv[:, LANES:] - ei[...] * conv[:, :LANES]) * (2.0 / (1024.0 * 4096.0))
+        back_send[...] = grad.reshape(8, 16, LANES)
     start(4)
     back_recv[me] = back_send[me]
 
@@ -390,7 +420,9 @@
 
 def finish(grad_ref, bins_ref, out_hbm, pg_hbm, pg_ref, sems):
     copies = [pltpu.make_async_copy(grad_ref, out_hbm, sems.at[0]), pltpu.make_async_copy(pg_ref, pg_hbm, sems.at[1])]
-    copies[0].start()
+    for k in range(4):
+        part = pl.ds(32 * k, 32)
+        pltpu.make_async_copy(grad_ref.at[part], out_hbm.at[part], sems.at[0]).start()
     pg_ref[0] = bins_ref[0, 0]
     pg_ref[1] = bins_ref[0, 1]
     copies[1].start()
@@ -419,7 +451,7 @@
             pltpu.VMEM((1, LANES), F32), pltpu.VMEM((1, LANES), F32),
             pltpu.VMEM((4, LANES, LANES), F32), pltpu.VMEM((4, LANES, 256), F32), pltpu.VMEM((2, 4, 64, LANES), F32),
             pltpu.VMEM((2, 256, LANES), F32), pltpu.VMEM((4, LANES, LANES), F32), pltpu.VMEM((4, 64, 256), F32),
-            pltpu.VMEM((2, 4, 64, LANES), F32),
+            pltpu.VMEM((4, 64, 256), BF16), pltpu.VMEM((4, 2, 32, LANES), F32),
             pltpu.VMEM((8, 4, 64, LANES), F32), pltpu.VMEM((8, 4, 64, LANES), F32),
             pltpu.VMEM((LANES, LANES), F32), pltpu.VMEM((LANES, LANES), F32),
             pltpu.VMEM((2, 4, 64, LANES), F32),

time: 29.5 us -> 29.5 us (level)
  no operation moved by 1% of the time
where the time goes in v4:
time: 29.5 us; the launch traced here: 29.4 us
  Pallas kernels  28.8 us (98%)
  between operations  0.64 us (2%)
    pallas_call x1, Pallas kernels, local(): pl.pallas_call(functools.partial(kernel, dims), out_shape=(pltpu.VMEM((LA...  28.1 us
    pallas_call x1, Pallas kernels, local(): pl.pallas_call(finish, out_shape=(jax.ShapeDtypeStruct((LANES, LANES), F3...  0.65 us

profile of v4, /device:TPU:1, one launch (start us, length us, event | category | flops | bytes accessed | tf_op | source)
XLA Modules:
  0.0 29.4 jit_solution(1637249737567914733)
XLA Ops:
  0.6 28.1 %shard_map.86 = (f32[128,128]{1,0:T(8,128)S(1)}, f32[1,128]{1,0:T(1,128)S(1)}) custom-call(bf16[512,128]{1,0:T(8,128)(2,1)} %cot_hbm.1, bf16[128,128]{1,0:T(8,128)(2,1)} %amp_hbm.1, f32[128,128]{1,0:T(8,128)} %ph_hbm.1, f32[2,128]{1,0:T(2,128)} %pos_hbm.1, f32[2]{0:T(128)} %prof_hbm.1, f32[2]{0:T(128)} %wt_hbm.1, bf16[3520,256]{1,0:T(8,128)(2,1)} %constant.2.clone.tab_hbm), custom_call_target="tpu_custom_call" | custom-call | tf_op jit(solution)/shard_map/pallas_call | solution.py:439
  28.8 0.7 %shard_map.87 = (f32[128,128]{1,0:T(8,128)}, f32[2]{0:T(128)}) custom-call(f32[128,128]{1,0:T(8,128)S(1)} %get-tuple-element.4.grad_ref, f32[1,128]{1,0:T(1,128)S(1)} %get-tuple-element.5.bins_ref), custom_call_target="tpu_custom_call" | custom-call | tf_op jit(solution)/shard_map/pallas_call | solution.py:462

commit v5 on v4

--- a/solution.py
+++ b/solution.py
@@ -232,8 +232,9 @@
         pltpu.make_async_copy(dst, dst, send_sem.at[kind]).wait()
 
     start(0)
-    start(1)
-    start(2)
+    for offset in order:
+        exchange(1, offset).start()
+        exchange(2, offset).start()
     start(3)
 
     small_recv[me] = small

time: 29.5 us -> 29.5 us (level)
  no operation moved by 1% of the time
where the time goes in v5:
time: 29.5 us; the launch traced here: 29.4 us
  Pallas kernels  28.7 us (97%)
  between operations  0.64 us (2%)
    pallas_call x1, Pallas kernels, local(): pl.pallas_call(functools.partial(kernel, dims), out_shape=(pltpu.VMEM((LA...  28.1 us
    pallas_call x1, Pallas kernels, local(): pl.pallas_call(finish, out_shape=(jax.ShapeDtypeStruct((LANES, LANES), F3...  0.65 us

profile of v5, /device:TPU:1, one launch (start us, length us, event | category | flops | bytes accessed | tf_op | source)
XLA Modules:
  0.0 29.4 jit_solution(801829199345087521)
XLA Ops:
  0.6 28.1 %shard_map.86 = (f32[128,128]{1,0:T(8,128)S(1)}, f32[1,128]{1,0:T(1,128)S(1)}) custom-call(bf16[512,128]{1,0:T(8,128)(2,1)} %cot_hbm.1, bf16[128,128]{1,0:T(8,128)(2,1)} %amp_hbm.1, f32[128,128]{1,0:T(8,128)} %ph_hbm.1, f32[2,128]{1,0:T(2,128)} %pos_hbm.1, f32[2]{0:T(128)} %prof_hbm.1, f32[2]{0:T(128)} %wt_hbm.1, bf16[3520,256]{1,0:T(8,128)(2,1)} %constant.2.clone.tab_hbm), custom_call_target="tpu_custom_call" | custom-call | tf_op jit(solution)/shard_map/pallas_call | solution.py:440
  28.7 0.7 %shard_map.87 = (f32[128,128]{1,0:T(8,128)}, f32[2]{0:T(128)}) custom-call(f32[128,128]{1,0:T(8,128)S(1)} %get-tuple-element.4.grad_ref, f32[1,128]{1,0:T(1,128)S(1)} %get-tuple-element.5.bins_ref), custom_call_target="tpu_custom_call" | custom-call | tf_op jit(solution)/shard_map/pallas_call | solution.py:463

commit v6 on v5

--- a/solution.py
+++ b/solution.py
@@ -404,6 +404,9 @@
     for k in range(4):
         grad_ref[32 * k : 32 * k + 32, :] = rows[k]
 
+    for kind in range(5):
+        wait_out(kind)
+    wait_all(column, st_a, sems_a.at[0])
     wait_all(plane, st_b, sems_b.at[1])
     stat = st_b[0]
     for k in range(1, ny * nx):
@@ -413,9 +416,6 @@
     own = [jnp.sum(jnp.where(lane[:1] == 2 * me + b, pg, 0.0), axis=1, keepdims=True) for b in range(2)]
     bins_ref[...] = jnp.where(lane[:1] == 0, own[0], own[1])
 
-    for kind in range(5):
-        wait_out(kind)
-    wait_all(column, st_a, sems_a.at[0])
     wait_all(plane, st_b, sems_b.at[0])
 
 

time: 29.5 us -> 29.5 us (level)
  no operation moved by 1% of the time
where the time goes in v6:
time: 29.5 us; the launch traced here: 29.4 us
  Pallas kernels  28.7 us (97%)
  between operations  0.64 us (2%)
    pallas_call x1, Pallas kernels, local(): pl.pallas_call(functools.partial(kernel, dims), out_shape=(pltpu.VMEM((LA...  28.1 us
    pallas_call x1, Pallas kernels, local(): pl.pallas_call(finish, out_shape=(jax.ShapeDtypeStruct((LANES, LANES), F3...  0.65 us

profile of v6, /device:TPU:1, one launch (start us, length us, event | category | flops | bytes accessed | tf_op | source)
XLA Modules:
  0.0 29.4 jit_solution(7905708670032131978)
XLA Ops:
  0.6 28.1 %shard_map.86 = (f32[128,128]{1,0:T(8,128)S(1)}, f32[1,128]{1,0:T(1,128)S(1)}) custom-call(bf16[512,128]{1,0:T(8,128)(2,1)} %cot_hbm.1, bf16[128,128]{1,0:T(8,128)(2,1)} %amp_hbm.1, f32[128,128]{1,0:T(8,128)} %ph_hbm.1, f32[2,128]{1,0:T(2,128)} %pos_hbm.1, f32[2]{0:T(128)} %prof_hbm.1, f32[2]{0:T(128)} %wt_hbm.1, bf16[3520,256]{1,0:T(8,128)(2,1)} %constant.2.clone.tab_hbm), custom_call_target="tpu_custom_call" | custom-call | tf_op jit(solution)/shard_map/pallas_call | solution.py:440
  28.7 0.7 %shard_map.87 = (f32[128,128]{1,0:T(8,128)}, f32[2]{0:T(128)}) custom-call(f32[128,128]{1,0:T(8,128)S(1)} %get-tuple-element.4.grad_ref, f32[1,128]{1,0:T(1,128)S(1)} %get-tuple-element.5.bins_ref), custom_call_target="tpu_custom_call" | custom-call | tf_op jit(solution)/shard_map/pallas_call | solution.py:463
